TPU v7x, 32 devices: a whole 2x2x4 slice. The times are simulated.
32 devices in a mesh: dp: 16 (over z, y, x), tensor: 2 (over core).
Axes of the slice: x: 2, y: 2, z: 4, core: 2. Of those that a mesh axis runs over, the one named last changes fastest.
Arguments:
- tokens: bfloat16 [25088, 768], P('dp'), may hold values from -6 to 6
- cotangent: bfloat16 [25088, 768], P('dp'), may hold values from -18 to 18
- w_qkv: bfloat16 [768, 3, 768], P(None, None, 'tensor'), may hold values from -0.21875 to 0.21875
- qv_bias: bfloat16 [2, 768], P(None, 'tensor'), may hold values from -3 to 3
- w_proj: bfloat16 [768, 768], P('tensor'), may hold values from -0.875 to 0.875
- proj_bias: bfloat16 [768], replicated, may hold values from -2 to 2
- w_fc1: bfloat16 [768, 3072], P(None, 'tensor'), may hold values from -0.21875 to 0.21875
- fc1_bias: bfloat16 [3072], P('tensor'), may hold values from -3 to 3
- w_fc2: bfloat16 [3072, 768], P('tensor'), may hold values from -0.109375 to 0.109375
- fc2_bias: bfloat16 [768], replicated, may hold values from -2 to 2
- gain_one: bfloat16 [768], replicated, may hold values from 0.5 to 1.5
- shift_one: bfloat16 [768], replicated, may hold values from -2 to 2
- gain_two: bfloat16 [768], replicated, may hold values from 0.5 to 1.5
- shift_two: bfloat16 [768], replicated, may hold values from -2 to 2
- rel_h: bfloat16 [27, 64], replicated, may hold values from -1 to 1
- rel_w: bfloat16 [27, 64], replicated, may hold values from -1 to 1
Outputs:
- output: bfloat16 [25088, 768], P('dp')
- d_tokens: bfloat16 [25088, 768], P('dp')
- d_w_qkv: float32 [768, 3, 768], P(None, None, 'tensor')
- d_qv_bias: float32 [2, 768], P(None, 'tensor')
- d_w_proj: float32 [768, 768], P('tensor')
- d_proj_bias: float32 [768], replicated
- d_w_fc1: float32 [768, 3072], P(None, 'tensor')
- d_fc1_bias: float32 [3072], P('tensor')
- d_w_fc2: float32 [3072, 768], P('tensor')
- d_fc2_bias: float32 [768], replicated
- d_gain_one: float32 [768], replicated
- d_shift_one: float32 [768], replicated
- d_gain_two: float32 [768], replicated
- d_shift_two: float32 [768], replicated
- d_rel_h: float32 [27, 64], replicated
- d_rel_w: float32 [27, 64], replicated
All inputs are finite; a program needn't handle non-finite values.
Results may differ from a plain program's by a relative error of at most 0.012.
The roundings to bfloat16 on the way count: a program that leaves them out, or rounds other values in their place, can miss the bound.
Values sent between devices are 32-bit elements; how exact they have to be, the bound alone decides.
No kernel may reach another device: no remote copies, remote signals or barrier semaphores. Data moves between devices by JAX's collectives and lax.ppermute only.
A program may use at most 256 MiB of HBM per device.

v0:
```python
import jax
import jax.numpy as jnp
from jax import lax
from jax.sharding import PartitionSpec as P

HEAD_DIM = 64
WIN = 14
IMG = 64
GRID = 5


NORM_EPS = 1e-06
PRECISE = lax.Precision.HIGHEST


def layer_norm(inputs, norm_gain, norm_shift):
    mean_val = jnp.mean(inputs, axis=-1, keepdims=True)
    centered = inputs - mean_val
    variance = jnp.mean(centered * centered, axis=-1, keepdims=True)
    return centered * lax.rsqrt(variance + NORM_EPS) * norm_gain + norm_shift


def gelu_exact(inputs):
    return 0.5 * inputs * (1.0 + jax.scipy.special.erf(inputs * 0.7071067811865476))


def row_mask(row_count, first_window):
    row_index = jnp.arange(row_count, dtype=jnp.int32)
    window = row_index // (WIN * WIN) + first_window
    inner_pos = row_index % (WIN * WIN)
    grid_cell = window % (GRID * GRID)
    row_pos = grid_cell // GRID * WIN + inner_pos // WIN
    col_pos = grid_cell % GRID * WIN + inner_pos % WIN
    return ((row_pos < IMG) & (col_pos < IMG)).astype(jnp.float32)[:, None]


def offset_table():
    near_index = jnp.arange(WIN, dtype=jnp.int32)
    offset_val = near_index[:, None] - near_index[None, :] + WIN - 1
    slots = jnp.arange(2 * WIN - 1, dtype=jnp.int32)
    return (offset_val[:, :, None] == slots[None, None, :]).astype(jnp.float32)


def attention_scores(q_six, k_four, table_h, table_w):
    win_count, head_count = (q_six.shape[0], q_six.shape[3])
    q_four = q_six.reshape(win_count, WIN * WIN, head_count, HEAD_DIM)
    base = jnp.einsum(
        "bqhc,bkhc->bhqk", q_four, k_four, preferred_element_type=jnp.float32
    ) * HEAD_DIM ** (-0.5)
    near_h = jnp.einsum("bijhc,ikc->bhijk", q_six, table_h, preferred_element_type=jnp.float32)
    near_w = jnp.einsum("bijhc,jlc->bhijl", q_six, table_w, preferred_element_type=jnp.float32)
    scores = (
        base.reshape(win_count, head_count, WIN, WIN, WIN, WIN)
        + near_h[..., :, None]
        + near_w[..., None, :]
    )
    return scores.reshape(win_count, head_count, WIN * WIN, WIN * WIN)


def shards(
    tokens,
    cotangent,
    w_qkv,
    qv_bias,
    w_proj,
    proj_bias,
    w_fc1,
    fc1_bias,
    w_fc2,
    fc2_bias,
    gain_one,
    shift_one,
    gain_two,
    shift_two,
    rel_h,
    rel_w,
):
    row_count = tokens.shape[0]
    win_count = row_count // (WIN * WIN)
    local_width = w_qkv.shape[2]
    head_count = local_width // HEAD_DIM
    first_window = lax.axis_index("dp") * win_count
    row_keep = row_mask(row_count, first_window)
    tok_wide = tokens.astype(jnp.float32)
    norm_gain_one = gain_one.astype(jnp.float32)
    norm_shift_one = shift_one.astype(jnp.float32)
    norm_gain_two = gain_two.astype(jnp.float32)
    norm_shift_two = shift_two.astype(jnp.float32)

    def norm_first(inputs, norm_gain, norm_shift):
        return row_keep * layer_norm(inputs, norm_gain, norm_shift)

    normed_one, norm_one_back = jax.vjp(norm_first, tok_wide, norm_gain_one, norm_shift_one)
    hidden_one = normed_one.astype(jnp.bfloat16)
    weight_qkv = w_qkv.reshape(w_qkv.shape[0], 3 * local_width)
    qkv = jnp.dot(hidden_one, weight_qkv, preferred_element_type=jnp.float32).reshape(
        row_count, 3, local_width
    )
    bias_wide = qv_bias.astype(jnp.float32)
    queries = (qkv[:, 0] + bias_wide[0]).astype(jnp.bfloat16)
    keys_low = qkv[:, 1].astype(jnp.bfloat16)
    values_low = (qkv[:, 2] + bias_wide[1]).astype(jnp.bfloat16)
    q_six = queries.reshape(win_count, WIN, WIN, head_count, HEAD_DIM)
    q_four = queries.reshape(win_count, WIN * WIN, head_count, HEAD_DIM)
    k_four = keys_low.reshape(win_count, WIN * WIN, head_count, HEAD_DIM)
    v_four = values_low.reshape(win_count, WIN * WIN, head_count, HEAD_DIM)
    one_hot = offset_table()
    table_h_wide = jnp.einsum("ikr,rc->ikc", one_hot, rel_h.astype(jnp.float32), precision=PRECISE)
    table_w_wide = jnp.einsum("ikr,rc->ikc", one_hot, rel_w.astype(jnp.float32), precision=PRECISE)
    table_h = table_h_wide.astype(jnp.bfloat16)
    table_w = table_w_wide.astype(jnp.bfloat16)
    scores = attention_scores(q_six, k_four, table_h, table_w)
    row_max = jnp.max(scores, axis=-1, keepdims=True)
    exp_terms = jnp.exp(scores - row_max)
    exp_total = jnp.sum(exp_terms, axis=-1, keepdims=True)
    log_total = row_max + jnp.log(exp_total)
    attn_probs = (exp_terms / exp_total).astype(jnp.bfloat16)
    context = jnp.einsum("bhqk,bkhc->bqhc", attn_probs, v_four, preferred_element_type=jnp.float32)
    context = context.reshape(row_count, local_width).astype(jnp.bfloat16)
    proj_part = jnp.dot(context, w_proj, preferred_element_type=jnp.float32)
    attention = lax.psum(proj_part, "tensor")
    y_one = tok_wide + attention + proj_bias.astype(jnp.float32)
    normed_two, norm_two_back = jax.vjp(layer_norm, y_one, norm_gain_two, norm_shift_two)
    hidden_two = normed_two.astype(jnp.bfloat16)
    pre_act = jnp.dot(hidden_two, w_fc1, preferred_element_type=jnp.float32) + fc1_bias.astype(
        jnp.float32
    )
    activation_wide, gelu_back = jax.vjp(gelu_exact, pre_act)
    activation = activation_wide.astype(jnp.bfloat16)
    fc2_part = jnp.dot(activation, w_fc2, preferred_element_type=jnp.float32)
    mlp_out = lax.psum(fc2_part, "tensor") + fc2_bias.astype(jnp.float32)
    output = (row_keep * (y_one + mlp_out)).astype(jnp.bfloat16)
    grad_out = row_keep * cotangent.astype(jnp.float32)
    grad_low = grad_out.astype(jnp.bfloat16)
    d_fc2_bias = jnp.sum(grad_out, axis=0)
    d_w_fc2 = jnp.einsum("rf,rd->fd", activation, grad_low, preferred_element_type=jnp.float32)
    d_act = jnp.einsum("rd,fd->rf", grad_low, w_fc2, preferred_element_type=jnp.float32)
    d_pre = gelu_back(d_act)[0].astype(jnp.bfloat16)
    d_w_fc1 = jnp.einsum("rd,rf->df", hidden_two, d_pre, preferred_element_type=jnp.float32)
    d_fc1_bias = jnp.sum(d_pre.astype(jnp.float32), axis=0)
    d_hidden_two_part = jnp.einsum("rf,df->rd", d_pre, w_fc1, preferred_element_type=jnp.float32)
    d_hidden_two = lax.psum(d_hidden_two_part, "tensor")
    d_y_norm, d_gain_two, d_shift_two = norm_two_back(d_hidden_two)
    d_y_one = grad_out + d_y_norm
    d_proj_bias = jnp.sum(d_y_one, axis=0)
    d_attn = d_y_one.astype(jnp.bfloat16)
    d_w_proj = jnp.einsum("rc,rd->cd", context, d_attn, preferred_element_type=jnp.float32)
    d_context = jnp.einsum("rd,cd->rc", d_attn, w_proj, preferred_element_type=jnp.float32).astype(
        jnp.bfloat16
    )
    d_ctx_four = d_context.reshape(win_count, WIN * WIN, head_count, HEAD_DIM)
    scores_again = attention_scores(q_six, k_four, table_h, table_w)
    soft_wide = jnp.exp(scores_again - log_total)
    soft_low = soft_wide.astype(jnp.bfloat16)
    d_probs = jnp.einsum("bqhc,bkhc->bhqk", d_ctx_four, v_four, preferred_element_type=jnp.float32)
    d_values = jnp.einsum(
        "bhqk,bqhc->bkhc", soft_low, d_ctx_four, preferred_element_type=jnp.float32
    )
    d_scores_wide = soft_wide * (d_probs - jnp.sum(d_probs * soft_wide, axis=-1, keepdims=True))
    d_scores = d_scores_wide.astype(jnp.bfloat16)
    d_scores_six = d_scores.reshape(win_count, head_count, WIN, WIN, WIN, WIN)
    d_near_h = jnp.sum(d_scores_six, axis=5, dtype=jnp.float32)
    d_near_w = jnp.sum(d_scores_six, axis=4, dtype=jnp.float32)
    d_q_base = jnp.einsum(
        "bhqk,bkhc->bqhc", d_scores, k_four, preferred_element_type=jnp.float32
    ) * HEAD_DIM ** (-0.5)
    d_q_rel = jnp.einsum("bhijk,ikc->bijhc", d_near_h, table_h_wide, precision=PRECISE)
    d_q_rel = d_q_rel + jnp.einsum("bhijl,jlc->bijhc", d_near_w, table_w_wide, precision=PRECISE)
    d_queries = (
        d_q_base.reshape(row_count, local_width) + d_q_rel.reshape(row_count, local_width)
    ).astype(jnp.bfloat16)
    d_keys = (
        (
            jnp.einsum("bhqk,bqhc->bkhc", d_scores, q_four, preferred_element_type=jnp.float32)
            * HEAD_DIM ** (-0.5)
        )
        .reshape(row_count, local_width)
        .astype(jnp.bfloat16)
    )
    d_values_low = d_values.reshape(row_count, local_width).astype(jnp.bfloat16)
    q_six_wide = q_six.astype(jnp.float32)
    d_table_h = jnp.einsum("bhijk,bijhc->ikc", d_near_h, q_six_wide, precision=PRECISE)
    d_table_w = jnp.einsum("bhijl,bijhc->jlc", d_near_w, q_six_wide, precision=PRECISE)
    d_rel_h_part = jnp.einsum("ikr,ikc->rc", one_hot, d_table_h, precision=PRECISE)
    d_rel_w_part = jnp.einsum("ikr,ikc->rc", one_hot, d_table_w, precision=PRECISE)
    d_qkv = jnp.stack((d_queries, d_keys, d_values_low), axis=1)
    d_w_qkv = jnp.einsum("rd,rtw->dtw", hidden_one, d_qkv, preferred_element_type=jnp.float32)
    d_qv_bias = jnp.stack(
        (
            jnp.sum(d_queries.astype(jnp.float32), axis=0),
            jnp.sum(d_values_low.astype(jnp.float32), axis=0),
        ),
        axis=0,
    )
    d_hidden_one_part = jnp.einsum("rtw,dtw->rd", d_qkv, w_qkv, preferred_element_type=jnp.float32)
    d_hidden_one, d_rel_h, d_rel_w = lax.psum(
        (d_hidden_one_part, d_rel_h_part, d_rel_w_part), "tensor"
    )
    d_tok_norm, d_gain_one, d_shift_one = norm_one_back(d_hidden_one)
    d_tokens = (d_y_one + d_tok_norm).astype(jnp.bfloat16)
    (
        d_w_qkv,
        d_qv_bias,
        d_w_proj,
        d_proj_bias,
        d_w_fc1,
        d_fc1_bias,
        d_w_fc2,
        d_fc2_bias,
        d_gain_one,
        d_shift_one,
        d_gain_two,
        d_shift_two,
        d_rel_h,
        d_rel_w,
    ) = lax.psum(
        (
            d_w_qkv,
            d_qv_bias,
            d_w_proj,
            d_proj_bias,
            d_w_fc1,
            d_fc1_bias,
            d_w_fc2,
            d_fc2_bias,
            d_gain_one,
            d_shift_one,
            d_gain_two,
            d_shift_two,
            d_rel_h,
            d_rel_w,
        ),
        "dp",
    )
    return (
        output,
        d_tokens,
        d_w_qkv,
        d_qv_bias,
        d_w_proj,
        d_proj_bias,
        d_w_fc1,
        d_fc1_bias,
        d_w_fc2,
        d_fc2_bias,
        d_gain_one,
        d_shift_one,
        d_gain_two,
        d_shift_two,
        d_rel_h,
        d_rel_w,
    )


def solution(mesh):
    return jax.shard_map(
        shards,
        mesh=mesh,
        in_specs=(
            P("dp", None),
            P("dp", None),
            P(None, None, "tensor"),
            P(None, "tensor"),
            P("tensor", None),
            P(),
            P(None, "tensor"),
            P("tensor"),
            P("tensor", None),
            P(),
            P(),
            P(),
            P(),
            P(),
            P(),
            P(),
        ),
        out_specs=(
            P("dp", None),
            P("dp", None),
            P(None, None, "tensor"),
            P(None, "tensor"),
            P("tensor", None),
            P(),
            P(None, "tensor"),
            P("tensor"),
            P("tensor", None),
            P(),
            P(),
            P(),
            P(),
            P(),
            P(),
            P(),
        ),
        check_vma=False,
    )
```

profile of v0, /device:TPU:0, one launch (start us, length us, event | category | flops | bytes accessed | tf_op | source)
XLA Modules:
  0.0 1091.0 jit_solution(10415210929864305501)
XLA Ops:
  70.0 8.9 fusion.33
  78.9 8.2 copy.135
  87.2 10.6 fusion.30
  97.8 7.9 copy.132
  105.7 27.3 %add.303 = f32[8,6,14,14,14,14]{5,4,0,3,2,1:T(8,128)} broadcast(f32[8,6,14,14,14]{4,0,3,2,1:T(8,128)} %copy.132), dimensions={0,1,2,3,4} | broadcast | bytes 7902720 | tf_op jit(solution)/shard_map/add | solution.py:53
  133.0 52.8 %add.304 = f32[8,6,196,196]{3,0,2,1:T(8,128)} reshape(f32[8,6,14,14,14,14]{5,4,0,3,2,1:T(8,128)} %add.303) | data formatting | bytes 14751744 | tf_op jit(solution)/shard_map/add | solution.py:53
  185.8 12.1 %copy.133 = f32[8,6,196,196]{2,3,1,0:T(8,128)} copy(f32[8,6,196,196]{3,0,2,1:T(8,128)} %add.304) | data formatting | bytes 14751744 | tf_op jit(solution)/shard_map/add | solution.py:53
  197.9 26.4 %add.306 = f32[8,6,14,14,14,14]{5,4,0,3,2,1:T(8,128)} broadcast(f32[8,6,14,14,14]{4,0,3,2,1:T(8,128)} %copy.135), dimensions={0,1,2,3,5} | broadcast | bytes 7902720 | tf_op jit(solution)/shard_map/add | solution.py:53
  224.3 52.8 %add.307 = f32[8,6,196,196]{3,0,2,1:T(8,128)} reshape(f32[8,6,14,14,14,14]{5,4,0,3,2,1:T(8,128)} %add.306) | data formatting | bytes 14751744 | tf_op jit(solution)/shard_map/add | solution.py:53
  277.2 12.1 %copy.136 = f32[8,6,196,196]{2,3,1,0:T(8,128)} copy(f32[8,6,196,196]{3,0,2,1:T(8,128)} %add.307) | data formatting | bytes 14751744 | tf_op jit(solution)/shard_map/add | solution.py:53
  293.0 8.3 fusion.121
  318.5 32.0 %all-reduce.9.cloned.1.call-done = f32[1568,768]{1,0:T(8,128)} async-done(((f32[1568,768]{1,0:T(8,128)}), f32[1568,768]{1,0:T(8,128)}) %all-reduce.9.cloned.1.call-update) | async-done | bytes 4816912 | tf_op jit(solution)/shard_map/psum | solution.py:121
  361.8 9.5 convert_reduce_fusion
  379.4 9.2 fusion.123
  388.6 21.2 %all-reduce.11.cloned.1.call-done = f32[1568,768]{1,0:T(8,128)} async-done(((f32[1568,768]{1,0:T(8,128)}), f32[1568,768]{1,0:T(8,128)}) %all-reduce.11.cloned.1.call-update) | async-done | bytes 4816912 | tf_op jit(solution)/shard_map/psum | solution.py:142
  445.7 11.2 %multiply_convert_fusion = bf16[8,6,196,196]{2,3,1,0:T(8,128)(2,1)} fusion(f32[8,6,196,196]{2,3,1,0:T(8,128)} %get-tuple-element.63, f32[8,6,196,196]{2,3,1,0:T(8,128)} %copy-done.2, f32[8,6,196]{2,1,0:T(8,128)S(1)} %get-tuple-element.62, f32[8,6,196]{2,1,0:T(8,128)S(1)} %log_add_fusion), kind=kLoop, calls=%fused_computation | loop fusion | flops 7375872 | bytes 18514944 | tf_op jit(solution)/shard_map/convert_element_type | solution.py:160
  462.1 9.1 copy.146
  489.5 48.8 %reshape.286 = f32[8,6,14,14,14,14]{5,4,0,3,2,1:T(8,128)} reshape(f32[8,6,196,196]{3,0,2,1:T(8,128)} %copy.146) | data formatting | bytes 14751744 | tf_op jit(solution)/shard_map/convert_element_type | solution.py:162
  538.2 29.7 %fusion.115 = (f32[8,6,14,14,14]{4,0,3,2,1:T(8,128)}, f32[8,6,14,14,14]{4,0,3,2,1:T(8,128)}) fusion(f32[8,6,14,14,14,14]{5,4,0,3,2,1:T(8,128)} %reshape.286), kind=kLoop, calls=%fused_computation.164 | loop fusion | flops 3424512 | bytes 8429568 | tf_op jit(solution)/shard_map/reduce_sum | solution.py:162
  622.7 10.1 fusion.66
  632.8 13.5 %fusion.113 = f32[768,1536]{1,0:T(8,128)} fusion(bf16[1568,1536]{1,0:T(8,128)(2,1)} %copy-done.64, f32[1568,768]{1,0:T(8,128)} %copy-done.3, f32[768]{0:T(1024)S(1)} %copy-done.57, f32[768]{0:T(1024)S(1)} %convert_element_type.191, f32[1568]{0:T(1024)S(1)} %fusion.110, f32[1568]{0:T(1024)S(1)} %broadcast_multiply_fusion), kind=kOutput, calls=%fused_computation.162 | convolution fusion | flops 3705397248 | bytes 14371072 | tf_op jit(solution)/shard_map/rd,rf->df/dot_general | solution.py:139
  676.4 9.5 fusion.15
  685.9 84.4 %all-reduce = (f32[2,384]{1,0:T(2,128)}, f32[768]{0:T(1024)}, f32[1536]{0:T(1024)}, f32[768]{0:T(1024)}, f32[768]{0:T(1024)}, /*index=5*/f32[768]{0:T(1024)}, f3...) all-reduce(f32[2,384]{1,0:T(2,128)S(1)} %pad_maximum_fusion.3, ...), channel_id=1, replica_groups=mesh['dp'=16,'tensor'=2] {'dp'}, use_global_device_ids=true, to_apply=%region_20.21 | all-reduce | flops 10368 | bytes 82944 | tf_op jit(solution)/shard_map/psum | solution.py:216
  781.8 291.6 %all-reduce.13.cloned.1.call-done = (f32[768,3,384]{2,0,1:T(8,128)}, f32[384,768]{1,0:T(8,128)}, f32[768,1536]{1,0:T(8,128)}, f32[1536,768]{1,0:T(8,128)}) async-done(((f32[768,3,384]{2,0,1:T(8,128)}, f32[384,768]{1,0:T(8,128)}, f32[768,1536]{1,0:T(8,128)}, f32[1536,768]{1,0:T(8,128)}), (f32[768,3,384]{2,0,1:T(8,128)}, f32[384,768]{1,0:T(8,128)}, f32[768,1536]{1,0:T(8,128)}, ...) | async-done | bytes 14155792 | tf_op jit(solution)/shard_map/psum | solution.py:216
  (241 shorter events, 269.0 us)
Async XLA Ops:
  7.2 348.0 %copy-start = (bf16[768,1536]{1,0:T(8,128)(2,1)S(1)}, bf16[768,1536]{1,0:T(8,128)(2,1)}, u32[]{:S(2)}) copy-start(bf16[768,1536]{1,0:T(8,128)(2,1)} %param.22) | copy-start | bytes 7077892
  7.2 343.3 %all-reduce.9.cloned.1.call-start = ((), (), s32[]{:S(2)}) async-start(), calls=%async_computation | async-start | bytes 9633792 | tf_op jit(solution)/shard_map/psum | solution.py:121
  7.3 29.0 %copy-start.36 = (s32[14,14]{1,0:T(8,128)}, s32[14,14]{1,0:T(8,128)S(1)}, u32[]{:S(2)}) copy-start(s32[14,14]{1,0:T(8,128)S(1)} %subtract_add_fusion) | copy-start | bytes 2356
  8.1 15.4 %copy-start.46 = (f32[768]{0:T(1024)}, f32[768]{0:T(1024)S(1)}, u32[]{:S(2)}) copy-start(f32[768]{0:T(1024)S(1)} %convert_element_type.176) | copy-start | bytes 9220
  8.8 14.8 %copy-start.54 = (f32[768]{0:T(1024)}, f32[768]{0:T(1024)S(1)}, u32[]{:S(2)}) copy-start(f32[768]{0:T(1024)S(1)} %convert_element_type.177) | copy-start | bytes 9220
  8.8 14.7 %copy-start.38 = (f32[1568]{0:T(1024)}, f32[1568]{0:T(1024)S(1)}, u32[]{:S(2)}) copy-start(f32[1568]{0:T(1024)S(1)} %and_convert_fusion) | copy-start | bytes 18820
  10.9 12.6 %copy-start.40 = (f32[1568]{0:T(1024)}, f32[1568]{0:T(1024)S(1)}, u32[]{:S(2)}) copy-start(f32[1568]{0:T(1024)S(1)} %broadcast_multiply_fusion.1) | copy-start | bytes 18820
  13.5 10.1 copy-start.44
  13.5 10.1 copy-start.42
  36.3 32.3 %copy-start.31 = (f32[14,14,64]{2,1,0:T(8,128)}, f32[14,14,64]{2,1,0:T(8,128)S(1)}, u32[]{:S(2)}) copy-start(f32[14,14,64]{2,1,0:T(8,128)S(1)} %fusion.73) | copy-start | bytes 150532
  36.5 50.7 %copy-start.33 = (f32[14,14,64]{2,1,0:T(8,128)}, f32[14,14,64]{2,1,0:T(8,128)S(1)}, u32[]{:S(2)}) copy-start(f32[14,14,64]{2,1,0:T(8,128)S(1)} %fusion.74) | copy-start | bytes 150532
  318.4 91.4 %all-reduce.11.cloned.1.call-start = ((), (), s32[]{:S(2)}) async-start(), calls=%async_computation.1 | async-start | bytes 9633792 | tf_op jit(solution)/shard_map/psum | solution.py:142
  318.5 36.7 %copy-start.56 = (f32[768]{0:T(1024)}, f32[768]{0:T(1024)S(1)}, u32[]{:S(2)}) copy-start(f32[768]{0:T(1024)S(1)} %convert_element_type.192) | copy-start | bytes 9220
  379.1 297.2 %all-reduce.15.cloned.1.call-start = ((), (), s32[]{:S(2)}) async-start(), calls=%async_computation.3 | async-start | bytes 19267584 | tf_op jit(solution)/shard_map/psum | solution.py:131
  445.7 11.2 %copy-start.13 = (bf16[8,196,6,64]{1,0,3,2:T(8,128)(2,1)S(1)}, bf16[8,196,6,64]{1,0,3,2:T(8,128)(2,1)}, u32[]{:S(2)}) copy-start(bf16[8,196,6,64]{1,0,3,2:T(8,128)(2,1)} %add_convert_fusion.4) | copy-start | bytes 3612676
  538.2 29.7 %copy-start.32 = (f32[14,14,64]{2,1,0:T(8,128)S(1)}, f32[14,14,64]{2,1,0:T(8,128)}, u32[]{:S(2)}) copy-start(f32[14,14,64]{2,1,0:T(8,128)} %copy-done.31) | copy-start | bytes 150532
  622.4 10.4 copy-start.57
  622.4 451.0 %all-reduce.13.cloned.1.call-start = ((), (), s32[]{:S(2)}) async-start(), calls=%async_computation.2 | async-start | bytes 28311552 | tf_op jit(solution)/shard_map/psum | solution.py:216
  622.7 23.6 %slice-start = ((s8[4816896]{0:T(1024)(128)(4,1)}), s8[4194304]{0:T(1024)(128)(4,1)S(1)}, s32[]{:S(2)}) async-start(s8[4816896]{0:T(1024)(128)(4,1)} %bitcast.110), calls=%async_computation.4 | async-start | bytes 8388608
  632.8 13.5 %slice-start.1 = ((s8[4816896]{0:T(1024)(128)(4,1)}), s8[622592]{0:T(1024)(128)(4,1)S(1)}, s32[]{:S(2)}) async-start(s8[4816896]{0:T(1024)(128)(4,1)} %bitcast.110), calls=%async_computation.5 | async-start | bytes 1245184
  632.8 13.5 %copy-start.16 = (bf16[1568,768]{1,0:T(8,128)(2,1)S(1)}, bf16[1568,768]{1,0:T(8,128)(2,1)}, u32[]{:S(2)}) copy-start(bf16[1568,768]{1,0:T(8,128)(2,1)} %param.17) | copy-start | bytes 7225348
  632.8 13.5 %copy-start.18 = (bf16[1568,384]{0,1:T(8,128)(2,1)S(1)}, bf16[1568,384]{0,1:T(8,128)(2,1)}, u32[]{:S(2)}) copy-start(bf16[1568,384]{0,1:T(8,128)(2,1)} %convert_element_type.189) | copy-start | bytes 3612676
  676.3 9.6 copy-start.48
  676.4 94.0 %copy-start.45 = (f32[1568]{0:T(1024)S(1)}, f32[1568]{0:T(1024)}, u32[]{:S(2)}) copy-start(f32[1568]{0:T(1024)} %copy-done.44) | copy-start | bytes 18820
  (51 other events, 244.9 us)
Sparse Core Ops, SparseCore 0:
  318.5 31.9 all-reduce.8
  379.2 30.4 all-reduce.10
  622.5 42.3 all-reduce.14
  672.4 401.0 all-reduce.12
where the time goes:
time: 1100 us; the launch traced here: 1090 us
  local copies, waits for them, and re-layouts  377 us (34%)
  waiting for transfers between devices  345 us (31%)
  matrix products  165 us (15%)
  other arithmetic  101 us (9%)
  blocking collectives  88.1 us (8%)
  between operations  14.8 us (1%)
    psum x1, waiting for transfers between devices, shards(): lax.psum((d_w_qkv, d_qv_bias, d_w_proj, d_proj_bias, d_w_fc1, d_fc1_bias,...  292 us
    add x6, local copies, waits for them, and re-layouts, attention_scores(): base.reshape(win_count, head_count, WIN, WIN, WIN, WIN)  184 us
    psum x1, blocking collectives, shards(): lax.psum((d_w_qkv, d_qv_bias, d_w_proj, d_proj_bias, d_w_fc1, d_fc1_bias,...  84.4 us
    convert_element_type x2, local copies, waits for them, and re-layouts, shards(): d_near_h = jnp.sum(d_scores_six, axis=5, dtype=jnp.float32)  57.8 us
    psum x1, waiting for transfers between devices, shards(): attention = lax.psum(proj_part, 'tensor')  32 us
    reduce_sum x1, other arithmetic, shards(): d_near_h = jnp.sum(d_scores_six, axis=5, dtype=jnp.float32)  29.7 us
    unnamed x147, local copies, waits for them, and re-layouts  25 us
  transfers between devices with their start and end apart: 4, of which 3 were waited for; matrix products, arithmetic and copies ran while one was open for 7% of the time, Pallas kernels for 0%

commit v1 on v0

v1 whole, which is shorter than its diff:
```python
import functools
import jax
import jax.numpy as jnp
from jax import lax
from jax.experimental import pallas as pl
from jax.experimental.pallas import tpu as pltpu
from jax.sharding import PartitionSpec as P

IMG = 64
GRID = 5

HEAD_DIM = 64
WIN = 14
TOK = WIN * WIN
PADW = 208
NEG = -1e30
EPS = 1e-6
SCALE = HEAD_DIM ** -0.5
NT = (((1,), (1,)), ((), ()))
TN = (((0,), (0,)), ((), ()))
NN = (((1,), (0,)), ((), ()))


def mm(a, b, dims=NN):
    return lax.dot_general(a, b, dims, preferred_element_type=jnp.float32)


def rel_matrix(rel_h, rel_w):
    pad = jnp.zeros((5, HEAD_DIM), rel_h.dtype)
    near = jnp.concatenate([rel_h[::-1], pad, rel_w[::-1], pad], 0)
    zero = jnp.zeros_like(near)
    return jnp.concatenate(
        [jnp.concatenate([zero, near.T], 1), jnp.concatenate([near.T, zero], 1)], 0
    )


def key_matrix():
    key = jnp.arange(PADW)[:, None]
    lane = jnp.arange(128)[None, :] % 64
    real = key < TOK
    slot = lane % 16
    hot = jnp.where(lane < 32, key // WIN == slot, key % WIN == slot) & real & (slot < WIN)
    once = hot & (lane % 32 < 16)
    neg = jnp.where((lane == 30) & ~real, NEG, 0.0)
    return (hot.astype(jnp.float32) + neg).astype(jnp.bfloat16), once.astype(jnp.bfloat16)


def shift_table():
    row = jnp.minimum(jnp.arange(PADW), TOK - 1)[:, None]
    lane = jnp.arange(128)[None, :] % 64
    return jnp.where(lane < 32, WIN - 1 - row // WIN, WIN - 1 - row % WIN).astype(jnp.int32)


def lanes():
    return lax.broadcasted_iota(jnp.int32, (PADW, 128), 1)


def fwd_kernel(x_ref, keep_ref, gain_ref, shift_ref, w_ref, bias_ref, rel_ref, hot_ref, tab_ref,
               hid_ref, qkv_ref, prob_ref, ctx_ref, acc_ref):
    x = x_ref[...].astype(jnp.float32)
    mean = jnp.mean(x, axis=1, keepdims=True)
    cen = x - mean
    var = jnp.mean(cen * cen, axis=1, keepdims=True)
    h = cen * lax.rsqrt(var + EPS) * gain_ref[...] + shift_ref[...]
    h = (h * keep_ref[...]).astype(jnp.bfloat16)
    hid_ref[...] = h
    width = w_ref.shape[2]
    for t in range(3):
        acc_ref[:, t * width:(t + 1) * width] = mm(h, w_ref[t]) + bias_ref[t:t + 1]
    lane = lanes()
    low_half = lane < 64
    slot = lane % 32
    near_ok = slot < WIN
    one_lane = lane % 64 == 30
    tab = tab_ref[...]
    bits = [(tab & (1 << b)) != 0 for b in range(4)]
    hot = hot_ref[...]
    for w in range(x_ref.shape[0] // TOK):
        rows = acc_ref[w * TOK:(w + 1) * TOK, :]
        qkv_ref[w, :TOK, :] = rows.astype(jnp.bfloat16)
        qkv_ref[w, TOK:, :] = jnp.zeros((PADW - TOK, 3 * width), jnp.bfloat16)
        for p in range(width // 128):
            q = qkv_ref[w, :, p * 128:(p + 1) * 128]
            k = qkv_ref[w, :, width + p * 128:width + (p + 1) * 128]
            v = qkv_ref[w, :, 2 * width + p * 128:2 * width + (p + 1) * 128]
            near = mm(q, rel_ref[...])
            for b in range(4):
                near = jnp.where(bits[b], pltpu.roll(near, 128 - (1 << b), 1), near)
            near = jnp.where(near_ok, near, 0.0)
            high = near.astype(jnp.bfloat16).astype(jnp.float32)
            both = high + pltpu.roll(near - high, 16, 1)
            both = jnp.where(one_lane, 1.0, both)
            qs = q.astype(jnp.float32) * SCALE
            xe = jnp.where(low_half, qs, both).astype(jnp.bfloat16)
            xo = jnp.where(low_half, both, qs).astype(jnp.bfloat16)
            ke = jnp.where(low_half, k, hot)
            ko = jnp.where(low_half, hot, k)
            outs = []
            for e, (xx, kk) in enumerate(((xe, ke), (xo, ko))):
                s = mm(xx, kk, NT)
                m = jnp.max(s, axis=1, keepdims=True)
                ex = jnp.exp(s - m)
                pr = (ex * (1.0 / jnp.sum(ex, axis=1, keepdims=True))).astype(jnp.bfloat16)
                prob_ref[w, 2 * p + e] = pr
                outs.append(mm(pr, v))
            out = jnp.where(low_half, outs[0], outs[1])
            ctx_ref[w * TOK:(w + 1) * TOK, p * 128:(p + 1) * 128] = out[:TOK].astype(ctx_ref.dtype)


def attention_forward(tokens, keep, gain, shift, w3, bias3, relm, hot, tab):
    rows, width = tokens.shape
    local = w3.shape[2]
    heads = local // HEAD_DIM
    step = 2 * TOK
    steps = rows // step
    full = lambda a: pl.BlockSpec(a.shape, lambda i: (0,) * a.ndim)
    return pl.pallas_call(
        fwd_kernel,
        grid=(steps,),
        in_specs=[
            pl.BlockSpec((step, width), lambda i: (i, 0)),
            pl.BlockSpec((step, 1), lambda i: (i, 0)),
            full(gain), full(shift), full(w3), full(bias3), full(relm), full(hot), full(tab),
        ],
        out_specs=[
            pl.BlockSpec((step, width), lambda i: (i, 0)),
            pl.BlockSpec((2, PADW, 3 * local), lambda i: (i, 0, 0)),
            pl.BlockSpec((2, heads, PADW, PADW), lambda i: (i, 0, 0, 0)),
            pl.BlockSpec((step, local), lambda i: (i, 0)),
        ],
        out_shape=[
            jax.ShapeDtypeStruct((rows, width), jnp.bfloat16),
            jax.ShapeDtypeStruct((2 * steps, PADW, 3 * local), jnp.bfloat16),
            jax.ShapeDtypeStruct((2 * steps, heads, PADW, PADW), jnp.bfloat16),
            jax.ShapeDtypeStruct((rows, local), jnp.float32),
        ],
        scratch_shapes=[pltpu.VMEM((step, 3 * local), jnp.float32)],
        compiler_params=pltpu.CompilerParams(vmem_limit_bytes=48 << 20),
        cost_estimate=pl.CostEstimate(
            flops=rows * 2 * (width * 3 * local + 4 * PADW * local),
            bytes_accessed=rows * width * 4 + rows * local * 12 + 2 * steps * heads * PADW * PADW * 2,
            transcendentals=rows * heads * PADW,
        ),
        name="attention_forward",
    )(tokens, keep, gain, shift, w3, bias3, relm, hot, tab)


def bwd_kernel(dctx_ref, qkv_ref, prob_ref, rel_ref, once_ref, tab_ref, dqkv_ref, drel_ref, pad_ref):
    @pl.when(pl.program_id(0) == 0)
    def _():
        drel_ref[...] = jnp.zeros_like(drel_ref)
        pad_ref[...] = jnp.zeros_like(pad_ref)

    width = dctx_ref.shape[1]
    lane = lanes()
    low_half = lane < 64
    tab = tab_ref[...]
    bits = [(tab & (1 << b)) != 0 for b in range(4)]
    once = once_ref[...]
    rel = rel_ref[...]
    for w in range(dctx_ref.shape[0] // TOK):
        pad_ref[:TOK, :] = dctx_ref[w * TOK:(w + 1) * TOK, :]
        for p in range(width // 128):
            q = qkv_ref[w, :, p * 128:(p + 1) * 128]
            k = qkv_ref[w, :, width + p * 128:width + (p + 1) * 128]
            v = qkv_ref[w, :, 2 * width + p * 128:2 * width + (p + 1) * 128]
            do32 = pad_ref[:, p * 128:(p + 1) * 128]
            do = do32.astype(jnp.bfloat16)
            qs = (q.astype(jnp.float32) * SCALE).astype(jnp.bfloat16)
            ks = (k.astype(jnp.float32) * SCALE).astype(jnp.bfloat16)
            dv, dk, dqx = [], [], []
            for e in range(2):
                mine = low_half if e == 0 else ~low_half
                pr = prob_ref[w, 2 * p + e]
                dp = mm(jnp.where(mine, do32, 0.0).astype(jnp.bfloat16), v, NT)
                dv.append(mm(pr, do, TN))
                p32 = pr.astype(jnp.float32)
                ds = (p32 * (dp - jnp.sum(dp * p32, axis=1, keepdims=True))).astype(jnp.bfloat16)
                dk.append(mm(ds, qs, TN))
                dqx.append(mm(ds, jnp.where(mine, ks, once)))
            near = jnp.where(low_half, dqx[1], dqx[0])
            for b in range(4):
                near = jnp.where(bits[b], pltpu.roll(near, 1 << b, 1), near)
            high = near.astype(jnp.bfloat16)
            rest = (near - high.astype(jnp.float32)).astype(jnp.bfloat16)
            dq = jnp.where(low_half, dqx[0], dqx[1]) + mm(high, rel, NT) + mm(rest, rel, NT)
            drel_ref[...] += mm(high, q, TN) + mm(rest, q, TN)
            for t, g in enumerate((dq, jnp.where(low_half, dk[0], dk[1]), jnp.where(low_half, dv[0], dv[1]))):
                dqkv_ref[t, w * TOK:(w + 1) * TOK, p * 128:(p + 1) * 128] = g[:TOK]


def attention_backward(dctx, qkv, prob, relm, once, tab):
    rows, local = dctx.shape
    heads = local // HEAD_DIM
    step = 2 * TOK
    steps = rows // step
    full = lambda a: pl.BlockSpec(a.shape, lambda i: (0,) * a.ndim)
    return pl.pallas_call(
        bwd_kernel,
        grid=(steps,),
        in_specs=[
            pl.BlockSpec((step, local), lambda i: (i, 0)),
            pl.BlockSpec((2, PADW, 3 * local), lambda i: (i, 0, 0)),
            pl.BlockSpec((2, heads, PADW, PADW), lambda i: (i, 0, 0, 0)),
            full(relm), full(once), full(tab),
        ],
        out_specs=[
            pl.BlockSpec((3, step, local), lambda i: (0, i, 0)),
            pl.BlockSpec((128, 128), lambda i: (0, 0)),
        ],
        out_shape=[
            jax.ShapeDtypeStruct((3, rows, local), jnp.float32),
            jax.ShapeDtypeStruct((128, 128), jnp.float32),
        ],
        scratch_shapes=[pltpu.VMEM((PADW, local), jnp.float32)],
        compiler_params=pltpu.CompilerParams(vmem_limit_bytes=48 << 20),
        cost_estimate=pl.CostEstimate(
            flops=rows * 2 * 12 * PADW * local,
            bytes_accessed=rows * local * 4 * 5 + 2 * steps * heads * PADW * PADW * 2,
            transcendentals=0,
        ),
        name="attention_backward",
    )(dctx, qkv, prob, relm, once, tab)


def split_rel(acc):
    near = acc[64:, :64] + acc[:64, 64:]
    return near[26::-1], near[58:31:-1]


def pos():
    i = lax.axis_index("dp")
    return i & 1, (i >> 1) & 1, i >> 2
PX = [(i, i ^ 1) for i in range(16)]
PY = [(i, i ^ 2) for i in range(16)]
PN = [(i, i ^ 4) for i in range(16)]
PF = [(i, i ^ 8) for i in range(16)]
pp = lambda a, perm: lax.ppermute(a, "dp", perm)
def ix(a, *ids):
    n = len(ids)
    s = lax.dynamic_slice(a, tuple(ids) + (0,) * (a.ndim - n), (1,) * n + a.shape[n:])
    return s.reshape(a.shape[n:])
def put(out, p, *ids):
    n = len(ids)
    return lax.dynamic_update_slice(out, p.reshape((1,) * n + p.shape), tuple(ids) + (0,) * p.ndim)
def rs_xy(g, x, y):
    d0 = pp(ix(g, 1 - x, 1 - y, 0), PX)
    d1 = pp(ix(g, 1 - x, 1 - y, 1), PY)
    X = ix(g, 1 - x, y); Y = ix(g, x, 1 - y)
    sx = jnp.stack([X[0], X[1] + d1]); sy = jnp.stack([Y[0] + d0, Y[1]])
    rx = pp(sx, PX); ry = pp(sy, PY)
    return [ix(g, x, y), rx, ry]
def ag_xy(c, x, y):
    rx = pp(c, PX); ry = pp(c, PY)
    d0 = pp(ry[0], PX); d1 = pp(rx[1], PY)
    out = jnp.zeros((2, 2) + c.shape, c.dtype)
    out = put(out, c, x, y); out = put(out, rx, 1 - x, y); out = put(out, ry, x, 1 - y)
    out = put(out, d0, 1 - x, 1 - y, 0); out = put(out, d1, 1 - x, 1 - y, 1)
    return out
def ar_z(terms, z):
    b0, b1 = z & 1, z >> 1
    sh = terms[0].shape
    t = [a.reshape(2, 2, -1, sh[-1]) for a in terms]
    send = sum(ix(a, 1 - b0) for a in t); keep = sum(ix(a, b0) for a in t)
    r = pp(send, PN)
    s2 = ix(keep, 1 - b1) + ix(r, 1 - b1); k2 = ix(keep, b1) + ix(r, b1)
    r2 = pp(s2, PF)
    c = k2 + r2
    o = pp(c, PF)
    h = jnp.zeros((2,) + c.shape, c.dtype)
    h = put(h, c, b1); h = put(h, o, 1 - b1)
    oh = pp(h, PN)
    w = jnp.zeros((2,) + h.shape, c.dtype)
    w = put(w, h, b0); w = put(w, oh, 1 - b0)
    return w.reshape(sh)
def allreduce(g):
    x, y, z = pos()
    R, C = g.shape
    g5 = g.reshape(2, 2, 2, R // 8, C)
    terms = rs_xy(g5, x, y)
    c = ar_z(terms, z)
    return ag_xy(c, x, y).reshape(R, C)


def row_mask(row_count, first_window):
    row_index = jnp.arange(row_count, dtype=jnp.int32)
    window = row_index // TOK + first_window
    inner = row_index % TOK
    cell = window % (GRID * GRID)
    row_pos = cell // GRID * WIN + inner // WIN
    col_pos = cell % GRID * WIN + inner % WIN
    return ((row_pos < IMG) & (col_pos < IMG)).astype(jnp.float32)[:, None]


def swap(a):
    return lax.optimization_barrier(swap_raw(a))


def swap_raw(a):
    return lax.ppermute(a, "tensor", [(0, 1), (1, 0)])


def norm_parts(x):
    mean = jnp.mean(x, axis=1, keepdims=True)
    cen = x - mean
    rstd = lax.rsqrt(jnp.mean(cen * cen, axis=1, keepdims=True) + EPS)
    return cen * rstd, rstd


def norm_back(d, hat, rstd, gain):
    dh = d * gain
    return rstd * (dh - jnp.mean(dh, axis=1, keepdims=True) - hat * jnp.mean(dh * hat, axis=1, keepdims=True))


def gelu(u):
    return 0.5 * u * (1.0 + lax.erf(u * 0.7071067811865476))


def gelu_slope(u):
    return 0.5 * (1.0 + lax.erf(u * 0.7071067811865476)) + u * jnp.exp(-0.5 * u * u) * 0.3989422804014327


def mlp_kernel(tok_ref, ctx_ref, oth_ref, wp_ref, wpo_ref, pb_ref, gain_ref, shift_ref, w1_ref, b1_ref,
               y_ref, hid_ref, pre_ref, act_ref, wpo16_ref):
    @pl.when(pl.program_id(0) == 0)
    def _():
        wpo16_ref[...] = wpo_ref[...].astype(jnp.bfloat16)

    proj = mm(ctx_ref[...].astype(jnp.bfloat16), wp_ref[...]) + mm(oth_ref[...].astype(jnp.bfloat16), wpo16_ref[...])
    y = tok_ref[...].astype(jnp.float32) + proj + pb_ref[...]
    y_ref[...] = y
    cen = y - jnp.mean(y, axis=1, keepdims=True)
    var = jnp.mean(cen * cen, axis=1, keepdims=True)
    h = (cen * lax.rsqrt(var + EPS) * gain_ref[...] + shift_ref[...]).astype(jnp.bfloat16)
    hid_ref[...] = h
    pre = mm(h, w1_ref[...]) + b1_ref[...]
    pre_ref[...] = pre
    act_ref[...] = gelu(pre).astype(jnp.bfloat16)


def mlp_forward(tokens, ctx, oth, wp, wpo, pb, gain, shift, w1, b1):
    rows, width = tokens.shape
    local, units = ctx.shape[1], w1.shape[1]
    step = 2 * TOK
    full = lambda a: pl.BlockSpec(a.shape, lambda i: (0,) * a.ndim)
    row = lambda n: pl.BlockSpec((step, n), lambda i: (i, 0))
    return pl.pallas_call(
        mlp_kernel,
        grid=(rows // step,),
        in_specs=[row(width), row(local), row(local), full(wp), full(wpo), full(pb), full(gain), full(shift), full(w1), full(b1)],
        out_specs=[row(width), row(width), row(units), row(units)],
        out_shape=[
            jax.ShapeDtypeStruct((rows, width), jnp.float32),
            jax.ShapeDtypeStruct((rows, width), jnp.bfloat16),
            jax.ShapeDtypeStruct((rows, units), jnp.float32),
            jax.ShapeDtypeStruct((rows, units), jnp.bfloat16),
        ],
        scratch_shapes=[pltpu.VMEM(wpo.shape, jnp.bfloat16)],
        compiler_params=pltpu.CompilerParams(vmem_limit_bytes=48 << 20),
        cost_estimate=pl.CostEstimate(
            flops=2 * rows * width * (2 * local + units),
            bytes_accessed=rows * (width * 8 + local * 8 + units * 6),
            transcendentals=rows * units,
        ),
        name="mlp_forward",
    )(tokens, ctx, oth, wp, wpo, pb, gain, shift, w1, b1)


def reduce_all(g):
    if lax.axis_size("dp") == 16:
        return allreduce(g)
    return lax.psum(g, "dp")


def shards(tokens, cotangent, w_qkv, qv_bias, w_proj, proj_bias, w_fc1, fc1_bias, w_fc2, fc2_bias,
           gain_one, shift_one, gain_two, shift_two, rel_h, rel_w):
    f32, bf16 = jnp.float32, jnp.bfloat16
    rows, width = tokens.shape
    local = w_qkv.shape[2]
    keep = row_mask(rows, lax.axis_index("dp") * (rows // TOK))
    g1, s1 = gain_one.astype(f32)[None], shift_one.astype(f32)[None]
    g2, s2 = gain_two.astype(f32)[None], shift_two.astype(f32)[None]
    w3 = jnp.transpose(w_qkv, (1, 0, 2))
    bias = qv_bias.astype(f32)
    bias3 = jnp.stack([bias[0], jnp.zeros_like(bias[0]), bias[1]])
    relm = rel_matrix(rel_h, rel_w)
    hot, once = key_matrix()
    tab = shift_table()
    other_proj = swap(w_proj.astype(f32))
    tok = tokens.astype(f32)

    hid1, qkv, prob, ctx = attention_forward(tokens, keep, g1, s1, w3, bias3, relm, hot, tab)
    ctx_other = swap(ctx)
    y_one, hid2, pre, act = mlp_forward(
        tokens, ctx, ctx_other, w_proj, other_proj, proj_bias.astype(f32)[None], g2, s2, w_fc1, fc1_bias.astype(f32)[None])
    ctx = ctx.astype(bf16)
    hat2, rstd2 = norm_parts(y_one)

    grad_out = keep * cotangent.astype(f32)
    grad_low = grad_out.astype(bf16)
    dw_fc2 = reduce_all(mm(act, grad_low, TN))
    d_act = mm(grad_low, w_fc2, NT)
    d_pre = (d_act * gelu_slope(pre)).astype(bf16)
    dw_fc1 = reduce_all(mm(hid2, d_pre, TN))
    d_fc1_bias = jnp.sum(d_pre.astype(f32), axis=0)
    d_fc2_bias = jnp.sum(grad_out, axis=0)

    part = mm(act, w_fc2)
    mlp = (part + swap(part)) + fc2_bias.astype(f32)
    output = (keep * (y_one + mlp)).astype(bf16)

    part = mm(d_pre, w_fc1, NT)
    d_hid2 = part + swap(part)
    d_gain_two = jnp.sum(d_hid2 * hat2, axis=0)
    d_shift_two = jnp.sum(d_hid2, axis=0)
    d_y = grad_out + norm_back(d_hid2, hat2, rstd2, g2)
    d_proj_bias = jnp.sum(d_y, axis=0)
    d_attn = d_y.astype(bf16)
    dw_proj = mm(ctx, d_attn, TN)
    d_ctx = mm(d_attn, w_proj, NT).astype(bf16).astype(f32)
    d_qkv, acc = attention_backward(d_ctx, qkv, prob, relm, once, tab)
    d_rel_h, d_rel_w = split_rel(acc)
    d_low = d_qkv.astype(bf16)
    dw_qkv = jnp.concatenate([mm(hid1, d_low[t], TN) for t in range(3)], 0)
    d_qv_bias = jnp.sum(d_low.astype(f32), axis=1)
    part = mm(d_low[0], w3[0], NT) + mm(d_low[1], w3[1], NT) + mm(d_low[2], w3[2], NT)
    d_hid1 = (part + swap(part)) * keep
    hat1, rstd1 = norm_parts(tok)
    d_tokens = (d_y + norm_back(d_hid1, hat1, rstd1, g1)).astype(bf16)
    masked = part * keep
    shared = jnp.concatenate([
        jnp.sum(masked * hat1, axis=0), jnp.sum(masked, axis=0), d_rel_h.reshape(-1), d_rel_w.reshape(-1)])
    shared = shared + swap(shared)
    small = jnp.concatenate([
        shared, d_gain_two, d_shift_two, d_proj_bias, d_fc2_bias,
        d_fc1_bias, d_qv_bias[0], d_qv_bias[2]])
    count = small.shape[0]
    small = jnp.pad(small, (0, 128 * width - count)).reshape(128, width)
    third = reduce_all(jnp.concatenate([dw_proj, small], 0))
    dw_proj, small = third[:local], third[local:].reshape(-1)[:count]
    dw_qkv = jnp.transpose(reduce_all(dw_qkv).reshape(3, width, local), (1, 0, 2))
    sizes = [width, width, rel_h.size, rel_w.size, width, width, width, width, fc1_bias.shape[0], local, local]
    cuts, at = [], 0
    for n in sizes:
        cuts.append(small[at:at + n])
        at += n
    (d_gain_one, d_shift_one, d_rel_h, d_rel_w, d_gain_two, d_shift_two, d_proj_bias, d_fc2_bias,
     d_fc1_bias, dq_bias, dv_bias) = cuts
    return (output, d_tokens, dw_qkv, jnp.stack([dq_bias, dv_bias]), dw_proj, d_proj_bias, dw_fc1, d_fc1_bias,
            dw_fc2, d_fc2_bias, d_gain_one, d_shift_one, d_gain_two, d_shift_two,
            d_rel_h.reshape(rel_h.shape), d_rel_w.reshape(rel_w.shape))


def solution(mesh):
    rows, rep = P("dp", None), P()
    ins = (rows, rows, P(None, None, "tensor"), P(None, "tensor"), P("tensor", None), rep, P(None, "tensor"),
           P("tensor"), P("tensor", None), rep, rep, rep, rep, rep, rep, rep)
    return jax.shard_map(shards, mesh=mesh, in_specs=ins, out_specs=ins, check_vma=False)
```

time: 1100 us -> 554 us (0.50)
  local copies, waits for them, and re-layouts: 377 us -> 52.4 us
  matrix products: 165 us -> 54.8 us
  waiting for transfers between devices: 345 us -> 238 us
  blocking collectives: 88.1 us -> 0 us
  Pallas kernels: 0 us -> 83.2 us
  starting transfers between devices: 0.59 us -> 53.9 us
  other arithmetic: 101 us -> 59.8 us
  between operations: 14.8 us -> 2.35 us
    psum x4 -> x0, waiting for transfers between devices: 345 us -> none  [the longest x1 292 us: shards(): lax.psum((d_w_qkv, d_qv_bias, d_w_proj, d_proj_bias, d_w_fc1, d_fc1_bias,...]
    ppermute x0 -> x54, waiting for transfers between devices: none -> 238 us  [the longest x48 238 us: pp = lambda a, perm: lax.ppermute(a, 'dp', perm)]
    add x9 -> x0, local copies, waits for them, and re-layouts: 188 us -> none  [the longest x6 184 us: attention_scores(): base.reshape(win_count, head_count, WIN, WIN, WIN, WIN)]
    dot_general x28 -> x13, matrix products: 165 us -> 54.8 us  [mm(): return lax.dot_general(a, b, dims, preferred_element_type=jnp.float32)]
    convert_element_type x10 -> x0, local copies, waits for them, and re-layouts: 91.4 us -> none  [the longest x2 57.8 us: shards(): d_near_h = jnp.sum(d_scores_six, axis=5, dtype=jnp.float32)]
    psum x2 -> x0, blocking collectives: 88.1 us -> none  [the longest x1 84.4 us: shards(): lax.psum((d_w_qkv, d_qv_bias, d_w_proj, d_proj_bias, d_w_fc1, d_fc1_bias,...]
    pallas_call x0 -> x3, Pallas kernels: none -> 83.2 us  [the longest x1 37.7 us: attention_forward(): pl.pallas_call(fwd_kernel, grid=(steps,), in_specs=[pl.BlockSpec((step, w...]
    ppermute x0 -> x54, starting transfers between devices: none -> 53.9 us  [the longest x48 52.9 us: pp = lambda a, perm: lax.ppermute(a, 'dp', perm)]
  transfers between devices with their start and end apart: 4 -> 54, of which waited for: 3 -> 36; matrix products, arithmetic and copies ran while one was open for 7% -> 24% of each run, Pallas kernels for 0% -> 6%
where the time goes in v1:
time: 554 us; the launch traced here: 545 us
  waiting for transfers between devices  238 us (43%)
  Pallas kernels  83.2 us (15%)
  other arithmetic  59.8 us (11%)
  matrix products  54.8 us (10%)
  starting transfers between devices  53.9 us (10%)
  local copies, waits for them, and re-layouts  52.4 us (9%)
    ppermute x48, waiting for transfers between devices, pp = lambda a, perm: lax.ppermute(a, 'dp', perm)  238 us
    dot_general x13, matrix products, mm(): return lax.dot_general(a, b, dims, preferred_element_type=jnp.float32)  54.8 us
    ppermute x48, starting transfers between devices, pp = lambda a, perm: lax.ppermute(a, 'dp', perm)  52.9 us
    pallas_call x1, Pallas kernels, attention_forward(): pl.pallas_call(fwd_kernel, grid=(steps,), in_specs=[pl.BlockSpec((step, w...  37.7 us
    pallas_call x1, Pallas kernels, attention_backward(): pl.pallas_call(bwd_kernel, grid=(steps,), in_specs=[pl.BlockSpec((step, l...  30.4 us
    dynamic_update_slice x32, local copies, waits for them, and re-layouts, put(): lax.dynamic_update_slice(out, p.reshape((1,) * n + p.shape), tuple(ids) +...  19.5 us
    pallas_call x1, Pallas kernels, mlp_forward(): pl.pallas_call(mlp_kernel, grid=(rows // step,), in_specs=[row(width), ro...  15.2 us
  transfers between devices with their start and end apart: 54, of which 36 were waited for; matrix products, arithmetic and copies ran while one was open for 24% of the time, Pallas kernels for 6%

profile of v1, /device:TPU:0, one launch (start us, length us, event | category | flops | bytes accessed | tf_op | source)
XLA Modules:
  0.0 544.7 jit_solution(7469481749098004024)
XLA Ops:
  11.7 37.7 %attention_forward.1 = (bf16[1568,768]{1,0:T(8,128)(2,1)S(1)}, bf16[8,208,1152]{2,1,0:T(8,128)(2,1)}, bf16[8,6,208,208]{3,2,1,0:T(8,128)(2,1)}, f32[1568,384]{1,0:T(8,128)}) custom-call(bf16[1568,768]{1,0:T(8,128)(2,1)} %tok_ref.1, f32[1568,1]{1,0:T(8,128)S(1)} %copy-done.5, f32[1,768]{1,0:T(1,128)S(1)} %broadcast_in_dim.128.gain_ref, ...), custom_call_target="tpu_custom_call" | custom-call | flops 3776446464 | bytes 16195584 | tf_op jit(solution)/shard_map/attention_forward/pallas_call | solution.py:117
  55.7 6.5 %fusion.36 = f32[1568,1536]{1,0:T(8,128)} fusion(bf16[1536,768]{1,0:T(8,128)(2,1)S(1)} %copy-done, bf16[1568,768]{1,0:T(8,128)(2,1)S(1)} %copy-done.15, f32[1568]{0:T(1024)S(1)} %and_convert_fusion.2), kind=kOutput, calls=%fused_computation.74 | convolution fusion | flops 3702988800 | bytes 14407808 | tf_op jit(solution)/shard_map/dot_general | solution.py:25
  62.2 15.2 %mlp_forward.1 = (f32[1568,768]{1,0:T(8,128)}, bf16[1568,768]{1,0:T(8,128)(2,1)}, f32[1568,1536]{1,0:T(8,128)}, bf16[1568,1536]{1,0:T(8,128)(2,1)}) custom-call(bf16[1568,768]{1,0:T(8,128)(2,1)} %tok_ref.1, f32[1568,384]{1,0:T(8,128)} %get-tuple-element.26.ctx_ref, f32[1568,384]{1,0:T(8,128)} %collective-permute-done.oth_ref, ...), custom_call_target="tpu_custom_call" | custom-call | flops 5549064192 | bytes 28901376 | tf_op jit(solution)/shard_map/mlp_forward/pallas_call | solution.py:347
  77.4 8.8 %convert_reduce_fusion = (f32[1536]{0:T(1024)S(1)}, bf16[1568,1536]{1,0:T(8,128)(2,1)S(1)}) fusion(f32[1568,1536]{1,0:T(8,128)} %fusion.36, f32[1568,1536]{1,0:T(8,128)} %get-tuple-element.29), kind=kLoop, calls=%fused_computation.7 | loop fusion | flops 28899840 | bytes 24090624 | tf_op jit(solution)/shard_map/reduce_sum | solution.py:405
  102.5 5.6 %collective-permute-done.30 = f32[96,1536]{1,0:T(8,128)S(1)} collective-permute-done((f32[96,1536]{1,0:T(8,128)S(1)}, f32[96,1536]{1,0:T(8,128)S(1)}, u32[]{:S(2)}, u32[]{:S(2)}) %collective-permute-start.30) | collective-permute-done | bytes 589856 | tf_op jit(solution)/shard_map/ppermute | solution.py:238
  127.0 19.1 %collective-permute-done.33 = f32[2,96,1536]{2,1,0:T(8,128)} collective-permute-done((f32[2,96,1536]{2,1,0:T(8,128)}, f32[2,96,1536]{2,1,0:T(8,128)}, u32[]{:S(2)}, u32[]{:S(2)}) %collective-permute-start.33) | collective-permute-done | bytes 1179680 | tf_op jit(solution)/shard_map/ppermute | solution.py:238
  151.8 19.5 %fusion.122 = f32[1568,768]{1,0:T(8,128)} fusion(bf16[1568,1536]{1,0:T(8,128)(2,1)} %copy-done.19, bf16[768,1536]{1,0:T(8,128)(2,1)S(1)} %copy-done.7), kind=kOutput, calls=%fused_computation.314 | convolution fusion | flops 3699376128 | bytes 11993088 | tf_op jit(solution)/shard_map/dot_general | solution.py:25
  186.0 8.1 %collective-permute-done.46 = f32[2,96,768]{2,1,0:T(8,128)} collective-permute-done((f32[2,96,768]{2,1,0:T(8,128)}, f32[2,96,768]{2,1,0:T(8,128)}, u32[]{:S(2)}, u32[]{:S(2)}) %collective-permute-start.46) | collective-permute-done | bytes 589856 | tf_op jit(solution)/shard_map/ppermute | solution.py:238
  199.7 17.9 %collective-permute-done.47 = f32[96,768]{1,0:T(8,128)S(1)} collective-permute-done((f32[96,768]{1,0:T(8,128)S(1)}, f32[96,768]{1,0:T(8,128)S(1)}, u32[]{:S(2)}, u32[]{:S(2)}) %collective-permute-start.47) | collective-permute-done | bytes 294944 | tf_op jit(solution)/shard_map/ppermute | solution.py:238
  218.8 11.5 %collective-permute-done.36 = f32[48,1536]{1,0:T(8,128)S(1)} collective-permute-done((f32[48,1536]{1,0:T(8,128)S(1)}, f32[48,1536]{1,0:T(8,128)S(1)}, u32[]{:S(2)}, u32[]{:S(2)}) %collective-permute-start.36) | collective-permute-done | bytes 294944 | tf_op jit(solution)/shard_map/ppermute | solution.py:238
  235.6 11.7 %collective-permute-done.37 = f32[2,48,1536]{2,1,0:T(8,128)S(1)} collective-permute-done((f32[2,48,1536]{2,1,0:T(8,128)S(1)}, f32[2,48,1536]{2,1,0:T(8,128)S(1)}, u32[]{:S(2)}, u32[]{:S(2)}) %collective-permute-start.37) | collective-permute-done | bytes 589856 | tf_op jit(solution)/shard_map/ppermute | solution.py:238
  252.8 7.0 %collective-permute-done.49 = f32[2,96,768]{2,1,0:T(8,128)S(1)} collective-permute-done((f32[2,96,768]{2,1,0:T(8,128)S(1)}, f32[2,96,768]{2,1,0:T(8,128)S(1)}, u32[]{:S(2)}, u32[]{:S(2)}) %collective-permute-start.49) | collective-permute-done | bytes 589856 | tf_op jit(solution)/shard_map/ppermute | solution.py:238
  265.2 11.1 %collective-permute-done.39 = f32[2,96,1536]{2,1,0:T(8,128)S(1)} collective-permute-done((f32[2,96,1536]{2,1,0:T(8,128)S(1)}, f32[2,96,1536]{2,1,0:T(8,128)S(1)}, u32[]{:S(2)}, u32[]{:S(2)}) %collective-permute-start.39) | collective-permute-done | bytes 1179680 | tf_op jit(solution)/shard_map/ppermute | solution.py:238
  282.4 18.1 %collective-permute-done.51 = f32[2,192,768]{2,1,0:T(8,128)S(1)} collective-permute-done((f32[2,192,768]{2,1,0:T(8,128)S(1)}, f32[2,192,768]{2,1,0:T(8,128)S(1)}, u32[]{:S(2)}, u32[]{:S(2)}) %collective-permute-start.51) | collective-permute-done | bytes 1179680 | tf_op jit(solution)/shard_map/ppermute | solution.py:238
  311.2 7.2 %fusion.115 = (f32[768]{0:T(1024)S(1)}, f32[1568,768]{1,0:T(8,128)S(1)}, bf16[1568,768]{1,0:T(8,128)(2,1)}) fusion(f32[1568]{0:T(1024)S(1)} %broadcast_multiply_fusion.3, f32[1568,768]{1,0:T(8,128)S(1)} %bitcast.314, f32[1568]{0:T(1024)S(1)} %broadcast_multiply_fusion.5, f32[1568]{0:T(1024)S(1)} %broadcast_multiply_fusion.4, ...), kind=kLoop, calls=%fused_computation.307 | loop fusion | flops 19266816 | bytes 28941952 | tf_op jit(solution)/shard_map/reduce_sum | solution.py:417
  319.9 30.4 %attention_backward.1 = (f32[3,1568,384]{2,1,0:T(8,128)}, f32[128,128]{1,0:T(8,128)S(1)}) custom-call(f32[1568,384]{1,0:T(8,128)S(1)} %fusion.20.dctx_ref, bf16[8,208,1152]{2,1,0:T(8,128)(2,1)} %get-tuple-element.30.qkv_ref, bf16[8,6,208,208]{3,2,1,0:T(8,128)(2,1)} %get-tuple-element.31.prob_ref, bf16[128,128]{1,0:T(8,128)(2,1)S(1)} %fusion.80.rel_ref, ...), custom_call_target="tpu_custom_call" | custom-call | flops 3005743104 | bytes 16195584 | tf_op jit(solution)/shard_map/attention_backward/pallas_call | solution.py:198
  377.9 13.6 %collective-permute-done.8 = f32[2,288,384]{2,1,0:T(8,128)S(1)} collective-permute-done((f32[2,288,384]{2,1,0:T(8,128)S(1)}, f32[2,288,384]{2,1,0:T(8,128)S(1)}, u32[]{:S(2)}, u32[]{:S(2)}) %collective-permute-start.8) | collective-permute-done | bytes 884768 | tf_op jit(solution)/shard_map/ppermute | solution.py:238
  396.1 9.4 %collective-permute-done.9 = f32[2,144,384]{2,1,0:T(8,128)S(1)} collective-permute-done((f32[2,144,384]{2,1,0:T(8,128)S(1)}, f32[2,144,384]{2,1,0:T(8,128)S(1)}, u32[]{:S(2)}, u32[]{:S(2)}) %collective-permute-start.9) | collective-permute-done | bytes 442400 | tf_op jit(solution)/shard_map/ppermute | solution.py:238
  407.4 9.1 %collective-permute-done.10 = f32[144,384]{1,0:T(8,128)S(1)} collective-permute-done((f32[144,384]{1,0:T(8,128)S(1)}, f32[144,384]{1,0:T(8,128)S(1)}, u32[]{:S(2)}, u32[]{:S(2)}) %collective-permute-start.10) | collective-permute-done | bytes 221216 | tf_op jit(solution)/shard_map/ppermute | solution.py:238
  416.9 9.1 %collective-permute-done.11 = f32[144,384]{1,0:T(8,128)S(1)} collective-permute-done((f32[144,384]{1,0:T(8,128)S(1)}, f32[144,384]{1,0:T(8,128)S(1)}, u32[]{:S(2)}, u32[]{:S(2)}) %collective-permute-start.11) | collective-permute-done | bytes 221216 | tf_op jit(solution)/shard_map/ppermute | solution.py:238
  455.9 7.5 %multiply_reduce_fusion.3 = (f32[768]{0:T(1024)S(1)}, f32[768]{0:T(1024)S(1)}, f32[768]{0:T(1024)S(1)}, f32[1568]{0:T(1024)S(1)}, f32[1568]{0:T(1024)S(1)}, /*index=5*/f32[1568,768]{1,0:T(8,128)}) fusion(f32[1568,768]{1,0:T(8,128)} %add_add_fusion, f32[1568]{0:T(1024)S(1)} %and_convert_fusion.2, f32[1568]{0:T(1024)S(1)} %add_rsqrt_fusion, ...), kind=kLoop, calls=%fused_computation.33 | loop fusion | flops 19262144 | bytes 19311232 | tf_op jit(solution)/shard_map/reduce_sum | solution.py:432
  471.0 11.3 %collective-permute-done.18 = f32[64,768]{1,0:T(8,128)S(1)} collective-permute-done((f32[64,768]{1,0:T(8,128)S(1)}, f32[64,768]{1,0:T(8,128)S(1)}, u32[]{:S(2)}, u32[]{:S(2)}) %collective-permute-start.18) | collective-permute-done | bytes 196640 | tf_op jit(solution)/shard_map/ppermute | solution.py:238
  501.7 6.1 %collective-permute-done.23 = f32[32,768]{1,0:T(8,128)S(1)} collective-permute-done((f32[32,768]{1,0:T(8,128)S(1)}, f32[32,768]{1,0:T(8,128)S(1)}, u32[]{:S(2)}, u32[]{:S(2)}) %collective-permute-start.23) | collective-permute-done | bytes 98336 | tf_op jit(solution)/shard_map/ppermute | solution.py:238
  508.0 6.3 %collective-permute-done.24 = f32[32,768]{1,0:T(8,128)S(1)} collective-permute-done((f32[32,768]{1,0:T(8,128)S(1)}, f32[32,768]{1,0:T(8,128)S(1)}, u32[]{:S(2)}, u32[]{:S(2)}) %collective-permute-start.24) | collective-permute-done | bytes 98336 | tf_op jit(solution)/shard_map/ppermute | solution.py:238
  (372 shorter events, 234.6 us)
Async XLA Ops:
  102.4 20.6 %collective-permute-start.44 = (f32[192,768]{1,0:T(8,128)}, f32[192,768]{1,0:T(8,128)}, u32[]{:S(2)}, u32[]{:S(2)}) collective-permute-start(f32[192,768]{1,0:T(8,128)} %get-tuple-element.70), channel_id=1, source_target_pairs={{0,2},{2,0},{4,6},{6,4},{8,10},{10,8},{12,14},{14,12},{16,18},{18,... | collective-permute-start | bytes 1769480 | tf_op jit(solution)/shard_map/ppermute | solution.py:238
  111.5 34.6 %collective-permute-start.33 = (f32[2,96,1536]{2,1,0:T(8,128)}, f32[2,96,1536]{2,1,0:T(8,128)}, u32[]{:S(2)}, u32[]{:S(2)}) collective-permute-start(f32[2,96,1536]{2,1,0:T(8,128)} %pad_maximum_fusion.3), channel_id=1, source_target_pairs={{0,4},{2,6},{4,0},{6,2},{8,12},{10,14},{12,8},{14,10},{16,20},{18,... | collective-permute-start | bytes 3538952 | tf_op jit(solution)/shard_map/ppermute | solution.py:238
  112.6 35.6 %collective-permute-start.31 = (f32[2,96,1536]{2,1,0:T(8,128)}, f32[2,96,1536]{2,1,0:T(8,128)}, u32[]{:S(2)}, u32[]{:S(2)}) collective-permute-start(f32[2,96,1536]{2,1,0:T(8,128)} %pad_maximum_fusion.2), channel_id=1, source_target_pairs={{0,2},{2,0},{4,6},{6,4},{8,10},{10,8},{12,14},{14,12},{16,18},{18,... | collective-permute-start | bytes 3538952 | tf_op jit(solution)/shard_map/ppermute | solution.py:238
  124.8 47.9 %collective-permute-start.45 = (f32[2,192,768]{2,1,0:T(8,128)S(1)}, f32[2,192,768]{2,1,0:T(8,128)S(1)}, u32[]{:S(2)}, u32[]{:S(2)}) collective-permute-start(f32[2,192,768]{2,1,0:T(8,128)S(1)} %pad_maximum_fusion.5), channel_id=1, source_target_pairs={{0,4},{2,6},{4,0},{6,2},{8,12},{10,14},{12,8},{14,10},{16,20},{18,... | collective-permute-start | bytes 3538952 | tf_op jit(solution)/shard_map/ppermute | solution.py:238
  125.0 47.7 %collective-permute-start.43 = (f32[2,192,768]{2,1,0:T(8,128)S(1)}, f32[2,192,768]{2,1,0:T(8,128)S(1)}, u32[]{:S(2)}, u32[]{:S(2)}) collective-permute-start(f32[2,192,768]{2,1,0:T(8,128)S(1)} %pad_maximum_fusion.4), channel_id=1, source_target_pairs={{0,2},{2,0},{4,6},{6,4},{8,10},{10,8},{12,14},{14,12},{16,18},{18,... | collective-permute-start | bytes 3538952 | tf_op jit(solution)/shard_map/ppermute | solution.py:238
  150.2 24.8 %collective-permute-start.34 = (f32[2,48,1536]{2,1,0:T(8,128)S(1)}, f32[2,48,1536]{2,1,0:T(8,128)S(1)}, u32[]{:S(2)}, u32[]{:S(2)}) collective-permute-start(f32[2,48,1536]{2,1,0:T(8,128)S(1)} %get-tuple-element.84), channel_id=1, source_target_pairs={{0,8},{2,10},{4,12},{6,14},{8,0},{10,2},{12,4},{14,6},{16,24},{18,... | collective-permute-start | bytes 1769480 | tf_op jit(solution)/shard_map/ppermute | solution.py:238
  173.9 20.1 %collective-permute-start.46 = (f32[2,96,768]{2,1,0:T(8,128)}, f32[2,96,768]{2,1,0:T(8,128)}, u32[]{:S(2)}, u32[]{:S(2)}) collective-permute-start(f32[2,96,768]{2,1,0:T(8,128)} %get-tuple-element.82), channel_id=1, source_target_pairs={{0,8},{2,10},{4,12},{6,14},{8,0},{10,2},{12,4},{14,6},{16,24},{18,... | collective-permute-start | bytes 1769480 | tf_op jit(solution)/shard_map/ppermute | solution.py:238
  175.0 21.8 %collective-permute-start.35 = (f32[48,1536]{1,0:T(8,128)S(1)}, f32[48,1536]{1,0:T(8,128)}, u32[]{:S(2)}, u32[]{:S(2)}) collective-permute-start(f32[48,1536]{1,0:T(8,128)S(1)} %fusion.71), channel_id=1, source_target_pairs={{0,16},{2,18},{4,20},{6,22},{8,24},{10,26},{12,28},{14,30},{16,0},... | collective-permute-start | bytes 884744 | tf_op jit(solution)/shard_map/ppermute | solution.py:238
  195.1 22.6 %collective-permute-start.47 = (f32[96,768]{1,0:T(8,128)S(1)}, f32[96,768]{1,0:T(8,128)S(1)}, u32[]{:S(2)}, u32[]{:S(2)}) collective-permute-start(f32[96,768]{1,0:T(8,128)S(1)} %fusion.70), channel_id=1, source_target_pairs={{0,16},{2,18},{4,20},{6,22},{8,24},{10,26},{12,28},{14,30},{16,0},... | collective-permute-start | bytes 884744 | tf_op jit(solution)/shard_map/ppermute | solution.py:238
  197.9 32.4 %collective-permute-start.36 = (f32[48,1536]{1,0:T(8,128)S(1)}, f32[48,1536]{1,0:T(8,128)S(1)}, u32[]{:S(2)}, u32[]{:S(2)}) collective-permute-start(f32[48,1536]{1,0:T(8,128)S(1)} %get-tuple-element.52), channel_id=1, source_target_pairs={{0,16},{2,18},{4,20},{6,22},{8,24},{10,26},{12,28},{14,30},{16,0},... | collective-permute-start | bytes 884744 | tf_op jit(solution)/shard_map/ppermute | solution.py:238
  199.2 109.0 %collective-permute-start.3 = (f32[1568,768]{1,0:T(8,128)}, f32[1568,768]{1,0:T(8,128)S(1)}, u32[]{:S(2)}, u32[]{:S(2)}) collective-permute-start(f32[1568,768]{1,0:T(8,128)} %fusion.122), channel_id=1, source_target_pairs={{0,1},{1,0},{2,3},{3,2},{4,5},{5,4},{6,7},{7,6},{8,9},{9,8},{10,11... | collective-permute-start | bytes 14450696 | tf_op jit(solution)/shard_map/ppermute | solution.py:300
  199.2 112.0 %collective-permute-start.2 = (f32[1568,768]{1,0:T(8,128)}, f32[1568,768]{1,0:T(8,128)}, u32[]{:S(2)}, u32[]{:S(2)}) collective-permute-start(f32[1568,768]{1,0:T(8,128)} %fusion.121), channel_id=1, source_target_pairs={{0,1},{1,0},{2,3},{3,2},{4,5},{5,4},{6,7},{7,6},{8,9},{9,8},{10,11... | collective-permute-start | bytes 14450696 | tf_op jit(solution)/shard_map/ppermute | solution.py:300
  234.7 25.1 %collective-permute-start.49 = (f32[2,96,768]{2,1,0:T(8,128)S(1)}, f32[2,96,768]{2,1,0:T(8,128)S(1)}, u32[]{:S(2)}, u32[]{:S(2)}) collective-permute-start(f32[2,96,768]{2,1,0:T(8,128)S(1)} %bitcast_dynamic-update-slice_fusion.20), channel_id=1, source_target_pairs={{0,8},{2,10},{4,12},{6,14},{8,0},{10,2},{12,4},{14,6},{16,24},{18,... | collective-permute-start | bytes 1769480 | tf_op jit(solution)/shard_map/ppermute | solution.py:238
  247.3 28.9 %collective-permute-start.39 = (f32[2,96,1536]{2,1,0:T(8,128)S(1)}, f32[2,96,1536]{2,1,0:T(8,128)S(1)}, u32[]{:S(2)}, u32[]{:S(2)}) collective-permute-start(f32[2,96,1536]{2,1,0:T(8,128)S(1)} %bitcast.335), channel_id=1, source_target_pairs={{0,4},{2,6},{4,0},{6,2},{8,12},{10,14},{12,8},{14,10},{16,20},{18,... | collective-permute-start | bytes 3538952 | tf_op jit(solution)/shard_map/ppermute | solution.py:238
  251.1 28.9 %collective-permute-start.38 = (f32[2,96,1536]{2,1,0:T(8,128)S(1)}, f32[2,96,1536]{2,1,0:T(8,128)S(1)}, u32[]{:S(2)}, u32[]{:S(2)}) collective-permute-start(f32[2,96,1536]{2,1,0:T(8,128)S(1)} %bitcast.336), channel_id=1, source_target_pairs={{0,2},{2,0},{4,6},{6,4},{8,10},{10,8},{12,14},{14,12},{16,18},{18,... | collective-permute-start | bytes 3538952 | tf_op jit(solution)/shard_map/ppermute | solution.py:238
  259.9 40.6 %collective-permute-start.51 = (f32[2,192,768]{2,1,0:T(8,128)S(1)}, f32[2,192,768]{2,1,0:T(8,128)S(1)}, u32[]{:S(2)}, u32[]{:S(2)}) collective-permute-start(f32[2,192,768]{2,1,0:T(8,128)S(1)} %bitcast.338), channel_id=1, source_target_pairs={{0,4},{2,6},{4,0},{6,2},{8,12},{10,14},{12,8},{14,10},{16,20},{18,... | collective-permute-start | bytes 3538952 | tf_op jit(solution)/shard_map/ppermute | solution.py:238
  276.3 29.0 %collective-permute-start.50 = (f32[2,192,768]{2,1,0:T(8,128)S(1)}, f32[2,192,768]{2,1,0:T(8,128)S(1)}, u32[]{:S(2)}, u32[]{:S(2)}) collective-permute-start(f32[2,192,768]{2,1,0:T(8,128)S(1)} %bitcast.340), channel_id=1, source_target_pairs={{0,2},{2,0},{4,6},{6,4},{8,10},{10,8},{12,14},{14,12},{16,18},{18,... | collective-permute-start | bytes 3538952 | tf_op jit(solution)/shard_map/ppermute | solution.py:238
  280.0 146.6 %collective-permute-start.40 = (f32[96,1536]{1,0:T(8,128)}, f32[96,1536]{1,0:T(8,128)}, u32[]{:S(2)}, u32[]{:S(2)}) collective-permute-start(f32[96,1536]{1,0:T(8,128)} %slice_bitcast_fusion.12), channel_id=1, source_target_pairs={{0,2},{2,0},{4,6},{6,4},{8,10},{10,8},{12,14},{14,12},{16,18},{18,... | collective-permute-start | bytes 1769480 | tf_op jit(solution)/shard_map/ppermute | solution.py:238
  300.5 142.7 %collective-permute-start.41 = (f32[96,1536]{1,0:T(8,128)}, f32[96,1536]{1,0:T(8,128)}, u32[]{:S(2)}, u32[]{:S(2)}) collective-permute-start(f32[96,1536]{1,0:T(8,128)} %slice_bitcast_fusion.11), channel_id=1, source_target_pairs={{0,4},{2,6},{4,0},{6,2},{8,12},{10,14},{12,8},{14,10},{16,20},{18,... | collective-permute-start | bytes 1769480 | tf_op jit(solution)/shard_map/ppermute | solution.py:238
  369.2 86.7 %collective-permute-start.4 = (f32[1568,768]{1,0:T(8,128)}, f32[1568,768]{1,0:T(8,128)}, u32[]{:S(2)}, u32[]{:S(2)}) collective-permute-start(f32[1568,768]{1,0:T(8,128)} %add_add_fusion), channel_id=1, source_target_pairs={{0,1},{1,0},{2,3},{3,2},{4,5},{5,4},{6,7},{7,6},{8,9},{9,8},{10,11... | collective-permute-start | bytes 14450696 | tf_op jit(solution)/shard_map/ppermute | solution.py:300
  374.0 20.4 %collective-permute-start.6 = (f32[2,288,384]{2,1,0:T(8,128)S(1)}, f32[2,288,384]{2,1,0:T(8,128)S(1)}, u32[]{:S(2)}, u32[]{:S(2)}) collective-permute-start(f32[2,288,384]{2,1,0:T(8,128)S(1)} %pad_maximum_fusion.6), channel_id=1, source_target_pairs={{0,2},{2,0},{4,6},{6,4},{8,10},{10,8},{12,14},{14,12},{16,18},{18,... | collective-permute-start | bytes 2654216 | tf_op jit(solution)/shard_map/ppermute | solution.py:238
  391.5 45.0 %collective-permute-start.52 = (f32[192,768]{1,0:T(8,128)}, f32[192,768]{1,0:T(8,128)}, u32[]{:S(2)}, u32[]{:S(2)}) collective-permute-start(f32[192,768]{1,0:T(8,128)} %slice_bitcast_fusion.10), channel_id=1, source_target_pairs={{0,2},{2,0},{4,6},{6,4},{8,10},{10,8},{12,14},{14,12},{16,18},{18,... | collective-permute-start | bytes 1769480 | tf_op jit(solution)/shard_map/ppermute | solution.py:238
  454.9 30.8 %collective-permute-start.15 = (f32[288,384]{1,0:T(8,128)}, f32[288,384]{1,0:T(8,128)}, u32[]{:S(2)}, u32[]{:S(2)}) collective-permute-start(f32[288,384]{1,0:T(8,128)} %slice_bitcast_fusion.20), channel_id=1, source_target_pairs={{0,2},{2,0},{4,6},{6,4},{8,10},{10,8},{12,14},{14,12},{16,18},{18,... | collective-permute-start | bytes 1327112 | tf_op jit(solution)/shard_map/ppermute | solution.py:238
  465.3 29.7 %collective-permute-start.16 = (f32[288,384]{1,0:T(8,128)}, f32[288,384]{1,0:T(8,128)}, u32[]{:S(2)}, u32[]{:S(2)}) collective-permute-start(f32[288,384]{1,0:T(8,128)} %slice_bitcast_fusion.19), channel_id=1, source_target_pairs={{0,4},{2,6},{4,0},{6,2},{8,12},{10,14},{12,8},{14,10},{16,20},{18,... | collective-permute-start | bytes 1327112 | tf_op jit(solution)/shard_map/ppermute | solution.py:238
  (81 other events, 1384.0 us)

commit v2 on v1

v2 whole, which is shorter than its diff:
```python
import jax
import jax.numpy as jnp
import numpy as np
from jax import lax
from jax.experimental import pallas as pl
from jax.experimental.pallas import tpu as pltpu
from jax.sharding import PartitionSpec as P

IMG = 64
GRID = 5
HEAD_DIM = 64
WIN = 14
TOK = WIN * WIN
PADW = 208
NEG = -1e30
EPS = 1e-6
SCALE = HEAD_DIM ** -0.5
NT = (((1,), (1,)), ((), ()))
TN = (((0,), (0,)), ((), ()))
NN = (((1,), (0,)), ((), ()))
F32, BF16 = jnp.float32, jnp.bfloat16


def mm(a, b, dims=NN):
    return lax.dot_general(a, b, dims, preferred_element_type=F32)


def full(a):
    return pl.BlockSpec(a.shape, lambda i: (0,) * a.ndim)


def rel_matrix(rel_h, rel_w):
    pad = jnp.zeros((5, HEAD_DIM), rel_h.dtype)
    near = jnp.concatenate([rel_h[::-1], pad, rel_w[::-1], pad], 0)
    zero = jnp.zeros_like(near)
    return jnp.concatenate(
        [jnp.concatenate([zero, near.T], 1), jnp.concatenate([near.T, zero], 1)], 0
    )


def key_matrix():
    key = np.arange(PADW)[:, None]
    lane = np.arange(128)[None, :] % 64
    real = key < TOK
    slot = lane % 32
    once = np.where(lane < 32, key // WIN == slot, key % WIN == slot) & real & (slot < WIN)
    neg = np.where((lane == 30) & ~real, NEG, 0.0)
    once = once.astype(np.float32)
    return jnp.asarray(once, BF16), jnp.asarray(once + neg, BF16)


def shift_table():
    row = np.minimum(np.arange(PADW), TOK - 1)[:, None]
    lane = np.arange(128)[None, :] % 64
    return jnp.asarray(np.where(lane < 32, WIN - 1 - row // WIN, WIN - 1 - row % WIN), jnp.int32)


def place_table():
    row = np.arange(2 * TOK) % TOK
    out = np.zeros((2 * TOK, 128), np.float32)
    out[:, 0], out[:, 1] = row // WIN, row % WIN
    return jnp.asarray(out)


def half_lanes():
    return lax.broadcasted_iota(jnp.int32, (PADW, 128), 1) < 64


def keep_rows(place, first):
    keeps = []
    for w in range(2):
        cell = lax.rem(first + w, GRID * GRID)
        top = (IMG - lax.div(cell, GRID) * WIN).astype(F32)
        left = (IMG - lax.rem(cell, GRID) * WIN).astype(F32)
        keeps.append((top, left))
    inner = lax.broadcasted_iota(jnp.int32, (2 * TOK, 1), 0) < TOK
    top = jnp.where(inner, keeps[0][0], keeps[1][0])
    left = jnp.where(inner, keeps[0][1], keeps[1][1])
    return jnp.where((place[:, 0:1] < top) & (place[:, 1:2] < left), 1.0, 0.0)


def fwd_kernel(first_ref, x_ref, cot_ref, place_ref, gain_ref, shift_ref, w_ref, bias_ref, rel_ref, hot_ref, once_ref,
               tab_ref, hid_ref, low_ref, qkv_ref, prob_ref, ctx_ref, sum_ref, acc_ref):
    step = pl.program_id(0)
    keep = keep_rows(place_ref[...], first_ref[0] + 2 * step)
    x = x_ref[...].astype(F32)
    cen = x - jnp.mean(x, axis=1, keepdims=True)
    var = jnp.mean(cen * cen, axis=1, keepdims=True)
    h = cen * lax.rsqrt(var + EPS) * gain_ref[...] + shift_ref[...]
    h = (h * keep).astype(BF16)
    hid_ref[...] = h
    low = cot_ref[...].astype(F32) * keep
    low_ref[...] = low.astype(BF16)

    @pl.when(step == 0)
    def _():
        sum_ref[...] = jnp.zeros_like(sum_ref)

    sum_ref[...] += jnp.sum(low, axis=0, keepdims=True)
    width = w_ref.shape[2]
    for t in range(3):
        acc_ref[:, t * width:(t + 1) * width] = mm(h, w_ref[t]) + bias_ref[t:t + 1]
    low_half = half_lanes()
    lane = lax.broadcasted_iota(jnp.int32, (PADW, 128), 1)
    one_lane = lane % 64 == 30
    hot, once = hot_ref[...], once_ref[...]
    zero = jnp.zeros_like(once)
    for w in range(2):
        qkv_ref[w, :TOK, :] = acc_ref[w * TOK:(w + 1) * TOK, :].astype(BF16)
        qkv_ref[w, TOK:, :] = jnp.zeros((PADW - TOK, 3 * width), BF16)
        for p in range(width // 128):
            q = qkv_ref[w, :, p * 128:(p + 1) * 128]
            k = qkv_ref[w, :, width + p * 128:width + (p + 1) * 128] * jnp.asarray(SCALE, BF16)
            v = qkv_ref[w, :, 2 * width + p * 128:2 * width + (p + 1) * 128]
            two = mm(q, rel_ref[...])
            tab = tab_ref[...]
            near = jnp.where((tab & 8) != 0, two[:, 128:], two[:, :128])
            for b in range(3):
                near = jnp.where((tab & (1 << b)) != 0, pltpu.roll(near, 128 - (1 << b), 1), near)
            high = near.astype(BF16)
            rest = (near - high.astype(F32)).astype(BF16)
            high = jnp.where(one_lane, jnp.ones_like(high), high)
            outs = []
            for e in range(2):
                mine = low_half if e == 0 else ~low_half
                xx = jnp.concatenate([jnp.where(mine, q, high), jnp.where(mine, zero, rest)], 1)
                kk = jnp.concatenate([jnp.where(mine, k, hot), jnp.where(mine, zero, once)], 1)
                s = mm(kk, xx, NT)
                ex = jnp.exp(s - jnp.max(s, axis=0, keepdims=True))
                pr = (ex * (1.0 / jnp.sum(ex, axis=0, keepdims=True))).astype(BF16)
                prob_ref[w, 2 * p + e] = pr
                outs.append(mm(pr, v, TN))
            out = jnp.where(low_half, outs[0], outs[1])
            ctx_ref[w * TOK:(w + 1) * TOK, p * 128:(p + 1) * 128] = out[:TOK]


def attention_forward(first, tokens, cot, place, gain, shift, w3, bias3, rel2, hot, once, tab):
    rows, width = tokens.shape
    local = w3.shape[2]
    heads = local // HEAD_DIM
    step = 2 * TOK
    steps = rows // step
    row = lambda n: pl.BlockSpec((step, n), lambda i: (i, 0))
    return pl.pallas_call(
        fwd_kernel,
        grid=(steps,),
        in_specs=[
            pl.BlockSpec(memory_space=pltpu.SMEM), row(width), row(width), full(place), full(gain), full(shift),
            full(w3), full(bias3), full(rel2), full(hot), full(once), full(tab),
        ],
        out_specs=[
            row(width), row(width),
            pl.BlockSpec((2, PADW, 3 * local), lambda i: (i, 0, 0)),
            pl.BlockSpec((2, heads, PADW, PADW), lambda i: (i, 0, 0, 0)),
            row(local),
            pl.BlockSpec((1, width), lambda i: (0, 0)),
        ],
        out_shape=[
            jax.ShapeDtypeStruct((rows, width), BF16),
            jax.ShapeDtypeStruct((rows, width), BF16),
            jax.ShapeDtypeStruct((2 * steps, PADW, 3 * local), BF16),
            jax.ShapeDtypeStruct((2 * steps, heads, PADW, PADW), BF16),
            jax.ShapeDtypeStruct((rows, local), F32),
            jax.ShapeDtypeStruct((1, width), F32),
        ],
        scratch_shapes=[pltpu.VMEM((step, 3 * local), F32)],
        compiler_params=pltpu.CompilerParams(vmem_limit_bytes=48 << 20),
        cost_estimate=pl.CostEstimate(
            flops=rows * 2 * (width * 3 * local + 4 * PADW * local),
            bytes_accessed=rows * width * 8 + rows * local * 12 + 2 * steps * heads * PADW * PADW * 2,
            transcendentals=rows * heads * PADW,
        ),
        name="attention_forward",
    )(first, tokens, cot, place, gain, shift, w3, bias3, rel2, hot, once, tab)


def bwd_kernel(dctx_ref, qkv_ref, prob_ref, rel_ref, once_ref, tab_ref, dqkv_ref, drel_ref, sum_ref, pad_ref, low_ref):
    @pl.when(pl.program_id(0) == 0)
    def _():
        drel_ref[...] = jnp.zeros_like(drel_ref)
        sum_ref[...] = jnp.zeros_like(sum_ref)
        pad_ref[...] = jnp.zeros_like(pad_ref)

    width = dctx_ref.shape[1]
    low_half = half_lanes()
    once = once_ref[...]
    rel2 = rel_ref[...]
    scale = jnp.asarray(SCALE, BF16)
    for w in range(2):
        pad_ref[:TOK, :] = dctx_ref[w * TOK:(w + 1) * TOK, :]
        for p in range(width // 128):
            q = qkv_ref[w, :, p * 128:(p + 1) * 128]
            k = qkv_ref[w, :, width + p * 128:width + (p + 1) * 128] * scale
            v = qkv_ref[w, :, 2 * width + p * 128:2 * width + (p + 1) * 128]
            qs = q * scale
            do = pad_ref[:, p * 128:(p + 1) * 128].astype(BF16)
            zero = jnp.zeros_like(do)
            dv, dk, dqx = [], [], []
            for e in range(2):
                mine = low_half if e == 0 else ~low_half
                pr = prob_ref[w, 2 * p + e]
                dp = mm(v, jnp.where(mine, do, zero), NT)
                dv.append(mm(pr, do))
                p32 = pr.astype(F32)
                ds = (p32 * (dp - jnp.sum(dp * p32, axis=0, keepdims=True))).astype(BF16)
                dk.append(mm(ds, qs))
                dqx.append(mm(ds, jnp.where(mine, k, once), TN))
            near = jnp.where(low_half, dqx[1], dqx[0])
            tab = tab_ref[...]
            for b in range(4):
                near = jnp.where((tab & (1 << b)) != 0, pltpu.roll(near, 1 << b, 1), near)
            high = near.astype(BF16)
            rest = (near - high.astype(F32)).astype(BF16)
            both = jnp.concatenate([high, rest], 1)
            dq = jnp.where(low_half, dqx[0], dqx[1]) + mm(both, rel2, NT)
            drel_ref[...] += mm(q, both, TN)
            for t, g in enumerate((dq, jnp.where(low_half, dk[0], dk[1]), jnp.where(low_half, dv[0], dv[1]))):
                low_ref[t, w * TOK:(w + 1) * TOK, p * 128:(p + 1) * 128] = g[:TOK]
    for t in range(3):
        g = low_ref[t].astype(BF16)
        dqkv_ref[t] = g
        sum_ref[t:t + 1, :] += jnp.sum(g.astype(F32), axis=0, keepdims=True)


def bwd_more_kernel(dctx_ref, qkv_ref, prob_ref, rel_ref, once_ref, tab_ref, _, *rest):
    bwd_kernel(dctx_ref, qkv_ref, prob_ref, rel_ref, once_ref, tab_ref, *rest)


def attention_backward(dctx, qkv, prob, rel2, once, tab, part, parts, done=None):
    rows, local = dctx.shape
    heads = local // HEAD_DIM
    step = 2 * TOK
    steps = rows // step // parts
    at = part * steps
    more = [] if done is None else [done]
    kernel = bwd_kernel if done is None else bwd_more_kernel
    return pl.pallas_call(
        kernel,
        grid=(steps,),
        input_output_aliases={} if done is None else {6: 0},
        in_specs=[
            pl.BlockSpec((step, local), lambda i: (i + at, 0)),
            pl.BlockSpec((2, PADW, 3 * local), lambda i: (i + at, 0, 0)),
            pl.BlockSpec((2, heads, PADW, PADW), lambda i: (i + at, 0, 0, 0)),
            full(rel2), full(once), full(tab),
        ] + [pl.BlockSpec(memory_space=pl.ANY) for _ in more],
        out_specs=[
            pl.BlockSpec((3, step, local), lambda i: (0, i + at, 0)),
            pl.BlockSpec((128, 256), lambda i: (0, 0)),
            pl.BlockSpec((8, local), lambda i: (0, 0)),
        ],
        out_shape=[
            jax.ShapeDtypeStruct((3, rows, local), BF16),
            jax.ShapeDtypeStruct((128, 256), F32),
            jax.ShapeDtypeStruct((8, local), F32),
        ],
        scratch_shapes=[pltpu.VMEM((PADW, local), F32), pltpu.VMEM((3, step, local), F32)],
        compiler_params=pltpu.CompilerParams(vmem_limit_bytes=48 << 20),
        cost_estimate=pl.CostEstimate(
            flops=steps * step * 2 * 12 * PADW * local,
            bytes_accessed=steps * step * local * 4 * 5 + 2 * steps * heads * PADW * PADW * 2,
            transcendentals=0,
        ),
        name="attention_backward",
    )(dctx, qkv, prob, rel2, once, tab, *more)


def split_rel(acc):
    acc = acc[:, :128] + acc[:, 128:]
    near = (acc[:64, 64:] + acc[64:, :64]).T
    return near[26::-1], near[58:31:-1]


def row_spec(n):
    return pl.BlockSpec((2 * TOK, n), lambda i: (i, 0))


def accumulate(ref, rows):
    @pl.when(pl.program_id(0) == 0)
    def _():
        ref[...] = jnp.zeros_like(ref)

    for i, r in enumerate(rows):
        ref[i:i + 1, :] += jnp.sum(r, axis=0, keepdims=True)


def mlp_half(h, low, w1, b1, w2, act_ref, pre_ref, sum_ref):
    u = mm(h, w1) + b1
    cdf = 0.5 * (1.0 + lax.erf(u * 0.7071067811865476))
    act_ref[...] = (u * cdf).astype(BF16)
    slope = cdf + u * jnp.exp(-0.5 * u * u) * 0.3989422804014327
    d = (mm(low, w2, NT) * slope).astype(BF16)
    pre_ref[...] = d
    accumulate(sum_ref, [d.astype(F32)])


def mlp_first_kernel(tok_ref, ctx_ref, oth_ref, low_ref, wp_ref, wpo_ref, pb_ref, gain_ref, shift_ref, w1_ref, b1_ref,
                     w2_ref, y_ref, hid_ref, act_ref, pre_ref, sum_ref, wpo16_ref):
    @pl.when(pl.program_id(0) == 0)
    def _():
        wpo16_ref[...] = wpo_ref[...].astype(BF16)

    proj = mm(ctx_ref[...].astype(BF16), wp_ref[...]) + mm(oth_ref[...].astype(BF16), wpo16_ref[...])
    y = tok_ref[...].astype(F32) + proj + pb_ref[...]
    y_ref[...] = y
    cen = y - jnp.mean(y, axis=1, keepdims=True)
    var = jnp.mean(cen * cen, axis=1, keepdims=True)
    h = (cen * lax.rsqrt(var + EPS) * gain_ref[...] + shift_ref[...]).astype(BF16)
    hid_ref[...] = h
    mlp_half(h, low_ref[...], w1_ref[...], b1_ref[...], w2_ref[...], act_ref, pre_ref, sum_ref)


def mlp_second_kernel(hid_ref, low_ref, w1_ref, b1_ref, w2_ref, act_ref, pre_ref, sum_ref):
    mlp_half(hid_ref[...], low_ref[...], w1_ref[...], b1_ref[...], w2_ref[...], act_ref, pre_ref, sum_ref)


def half_weight_specs(width, units, part):
    return [
        pl.BlockSpec((width, units), lambda i: (0, part)),
        pl.BlockSpec((1, units), lambda i: (0, part)),
        pl.BlockSpec((units, width), lambda i: (part, 0)),
    ]


def mlp_first(tokens, ctx, oth, low, wp, wpo, pb, gain, shift, w1, b1, w2):
    rows, width = tokens.shape
    local, units = ctx.shape[1], w1.shape[1] // 2
    return pl.pallas_call(
        mlp_first_kernel,
        grid=(rows // (2 * TOK),),
        in_specs=[row_spec(width), row_spec(local), row_spec(local), row_spec(width), full(wp), full(wpo), full(pb),
                  full(gain), full(shift)] + half_weight_specs(width, units, 0),
        out_specs=[row_spec(width), row_spec(width), row_spec(units), row_spec(units),
                   pl.BlockSpec((1, units), lambda i: (0, 0))],
        out_shape=[
            jax.ShapeDtypeStruct((rows, width), F32),
            jax.ShapeDtypeStruct((rows, width), BF16),
            jax.ShapeDtypeStruct((rows, units), BF16),
            jax.ShapeDtypeStruct((rows, units), BF16),
            jax.ShapeDtypeStruct((1, units), F32),
        ],
        scratch_shapes=[pltpu.VMEM(wpo.shape, BF16)],
        compiler_params=pltpu.CompilerParams(vmem_limit_bytes=48 << 20),
        cost_estimate=pl.CostEstimate(
            flops=2 * rows * width * (2 * local + 2 * units),
            bytes_accessed=rows * (width * 10 + local * 8 + units * 4), transcendentals=rows * units),
        name="mlp_first",
    )(tokens, ctx, oth, low, wp, wpo, pb, gain, shift, w1, b1, w2)


def mlp_second(hid, low, w1, b1, w2):
    rows, width = hid.shape
    units = w1.shape[1] // 2
    return pl.pallas_call(
        mlp_second_kernel,
        grid=(rows // (2 * TOK),),
        in_specs=[row_spec(width), row_spec(width)] + half_weight_specs(width, units, 1),
        out_specs=[row_spec(units), row_spec(units), pl.BlockSpec((1, units), lambda i: (0, 0))],
        out_shape=[
            jax.ShapeDtypeStruct((rows, units), BF16),
            jax.ShapeDtypeStruct((rows, units), BF16),
            jax.ShapeDtypeStruct((1, units), F32),
        ],
        compiler_params=pltpu.CompilerParams(vmem_limit_bytes=48 << 20),
        cost_estimate=pl.CostEstimate(
            flops=2 * rows * width * 2 * units, bytes_accessed=rows * (width * 4 + units * 4),
            transcendentals=rows * units),
        name="mlp_second",
    )(hid, low, w1, b1, w2)


def norm_back(d, hat, rstd, gain):
    dh = d * gain
    return rstd * (dh - jnp.mean(dh, axis=1, keepdims=True) - hat * jnp.mean(dh * hat, axis=1, keepdims=True))


def norm_parts(x):
    cen = x - jnp.mean(x, axis=1, keepdims=True)
    rstd = lax.rsqrt(jnp.mean(cen * cen, axis=1, keepdims=True) + EPS)
    return cen * rstd, rstd


def norm_two_kernel(part_ref, oth_ref, y_ref, low_ref, gain_ref, wp_ref, dy_ref, attn_ref, dctx_ref, sum_ref):
    d = part_ref[...] + oth_ref[...]
    hat, rstd = norm_parts(y_ref[...])
    dy = low_ref[...].astype(F32) + norm_back(d, hat, rstd, gain_ref[...])
    dy_ref[...] = dy
    low = dy.astype(BF16)
    attn_ref[...] = low
    dctx_ref[...] = mm(low, wp_ref[...], NT)
    accumulate(sum_ref, [d * hat, d, dy])


def norm_two_back(part, oth, y, low, gain, wp):
    rows, width = y.shape
    local = wp.shape[0]
    return pl.pallas_call(
        norm_two_kernel,
        grid=(rows // (2 * TOK),),
        in_specs=[row_spec(width)] * 4 + [full(gain), full(wp)],
        out_specs=[row_spec(width), row_spec(width), row_spec(local), pl.BlockSpec((8, width), lambda i: (0, 0))],
        out_shape=[
            jax.ShapeDtypeStruct((rows, width), F32),
            jax.ShapeDtypeStruct((rows, width), BF16),
            jax.ShapeDtypeStruct((rows, local), F32),
            jax.ShapeDtypeStruct((8, width), F32),
        ],
        compiler_params=pltpu.CompilerParams(vmem_limit_bytes=48 << 20),
        cost_estimate=pl.CostEstimate(
            flops=2 * rows * width * local, bytes_accessed=rows * (width * 20 + local * 4), transcendentals=0),
        name="norm_two_back",
    )(part, oth, y, low, gain, wp)


def norm_one_kernel(first_ref, part_ref, oth_ref, tok_ref, dy_ref, place_ref, gain_ref, dtok_ref, sum_ref):
    keep = keep_rows(place_ref[...], first_ref[0] + 2 * pl.program_id(0))
    d = (part_ref[...] + oth_ref[...]) * keep
    hat, rstd = norm_parts(tok_ref[...].astype(F32))
    dtok_ref[...] = (dy_ref[...] + norm_back(d, hat, rstd, gain_ref[...])).astype(BF16)
    accumulate(sum_ref, [d * hat, d])


def norm_one_back(first, part, oth, tokens, dy, place, gain):
    rows, width = tokens.shape
    return pl.pallas_call(
        norm_one_kernel,
        grid=(rows // (2 * TOK),),
        in_specs=[pl.BlockSpec(memory_space=pltpu.SMEM)] + [row_spec(width)] * 4 + [full(place), full(gain)],
        out_specs=[row_spec(width), pl.BlockSpec((8, width), lambda i: (0, 0))],
        out_shape=[jax.ShapeDtypeStruct((rows, width), BF16), jax.ShapeDtypeStruct((8, width), F32)],
        compiler_params=pltpu.CompilerParams(vmem_limit_bytes=48 << 20),
        cost_estimate=pl.CostEstimate(flops=rows * width * 20, bytes_accessed=rows * width * 16, transcendentals=0),
        name="norm_one_back",
    )(first, part, oth, tokens, dy, place, gain)


def output_kernel(first_ref, part_ref, oth_ref, y_ref, place_ref, bias_ref, out_ref):
    keep = keep_rows(place_ref[...], first_ref[0] + 2 * pl.program_id(0))
    mlp = (part_ref[...] + oth_ref[...]) + bias_ref[...]
    out_ref[...] = (keep * (y_ref[...] + mlp)).astype(BF16)


def block_output(first, part, oth, y, place, bias):
    rows, width = y.shape
    return pl.pallas_call(
        output_kernel,
        grid=(rows // (2 * TOK),),
        in_specs=[pl.BlockSpec(memory_space=pltpu.SMEM)] + [row_spec(width)] * 3 + [full(place), full(bias)],
        out_specs=row_spec(width),
        out_shape=jax.ShapeDtypeStruct((rows, width), BF16),
        compiler_params=pltpu.CompilerParams(vmem_limit_bytes=48 << 20),
        cost_estimate=pl.CostEstimate(flops=rows * width * 4, bytes_accessed=rows * width * 14, transcendentals=0),
        name="block_output",
    )(first, part, oth, y, place, bias)


def wait_for(arrays, token):
    return arrays if token is None else lax.optimization_barrier((arrays, token))[0]


def hold(arrays):
    return lax.optimization_barrier(arrays)


def send(a, stride):
    n = lax.axis_size("dp")
    return lax.ppermute(a, "dp", [(i, i ^ stride) for i in range(n)])


def pick(a, *ids):
    n = len(ids)
    return lax.dynamic_slice(a, tuple(ids) + (0,) * (a.ndim - n), (1,) * n + a.shape[n:]).reshape(a.shape[n:])


def put(out, piece, *ids):
    n = len(ids)
    return lax.dynamic_update_slice(out, piece.reshape((1,) * n + piece.shape), tuple(ids) + (0,) * piece.ndim)


def both(b, a, c):
    out = jnp.zeros((2,) + a.shape, a.dtype)
    return put(put(out, a, b), c, 1 - b)


class Plane:
    def __init__(self, g, bits, home):
        self.x, self.y, self.b0, self.b1 = bits
        self.rows, self.cols = g.shape
        self.home = home
        self.live = self.start(g)

    def start(self, g):
        return (g.reshape(2, 2, 2, self.rows // 8, self.cols),)

    def step(self, name, token):
        self.live, token = getattr(self, name)(*wait_for(self.live, token))
        return token

    def s1(self, g):
        x, y = self.x, self.y
        d0, d1 = hold((pick(g, 1 - x, 1 - y, 0), pick(g, 1 - x, 1 - y, 1)))
        return (g, send(d0, 1), send(d1, 2)), d0

    def s2(self, g, d0, d1):
        x, y = self.x, self.y
        to_x, to_y = pick(g, 1 - x, y), pick(g, x, 1 - y)
        to_x = jnp.concatenate([to_x[:1], to_x[1:] + d1[None]])
        to_y = jnp.concatenate([to_y[:1] + d0[None], to_y[1:]])
        to_x, to_y = hold((to_x, to_y))
        return (g, send(to_x, 1), send(to_y, 2)), to_x

    def z1(self, g, rx, ry):
        own = pick(g, self.x, self.y)
        b = self.b0
        out = pick(own, 1 - b) + pick(rx, 1 - b) + pick(ry, 1 - b)
        keep = pick(own, b) + pick(rx, b) + pick(ry, b)
        out, keep = hold((out, keep))
        return (keep, send(out, 4)), out

    def split(self, a):
        h, c = a.shape
        return a.reshape(2, h // 2, c) if h % 16 == 0 else a.reshape(h, 2, c // 2).transpose(1, 0, 2)

    def z2(self, keep, r):
        keep, r, b = self.split(keep), self.split(r), self.b1
        out = pick(keep, 1 - b) + pick(r, 1 - b)
        keep = pick(keep, b) + pick(r, b)
        out, keep = hold((out, keep))
        return (keep, send(out, 8)), out

    def z3(self, keep, r):
        c = hold(keep + r)
        return (c, send(c, 8)), c

    def z4(self, c, o):
        h = both(self.b1, c, o)
        n = self.rows // 8
        h = h.reshape(n, self.cols) if n % 16 == 0 else h.transpose(1, 0, 2).reshape(n, self.cols)
        h = hold(h)
        return (h, send(h, 4)), h

    def g1(self, h, o):
        w = hold(both(self.b0, h, o))
        return (w, send(w, 1), send(w, 2)), w

    def g2(self, w, rx, ry):
        a, b = hold((ry[0], rx[1]))
        return (w, rx, ry, send(a, 1), send(b, 2)), a

    def gather(self, out, w, rx, ry, d0, d1, row0, col0):
        x, y = self.x, self.y
        slab = w.shape[0] * w.shape[1]
        for piece, px, py, off in ((w, x, y, 0), (rx, 1 - x, y, 0), (ry, x, 1 - y, 0),
                                   (d0, 1 - x, 1 - y, 0), (d1, 1 - x, 1 - y, slab // 2)):
            piece = piece.reshape(-1, piece.shape[-1])
            out = lax.dynamic_update_slice(out, piece, (row0 + (2 * px + py) * slab + off, col0))
        return out

    def end(self, w, rx, ry, d0, d1):
        bufs, name, row0, col0 = self.home
        bufs[name] = hold(self.gather(bufs[name], w, rx, ry, d0, d1, row0, col0))
        return (), bufs[name]


class Column(Plane):
    def start(self, g):
        return (g.reshape(2, 2, self.rows // 4, self.cols),)

    def z1(self, g):
        out = hold(pick(g, 1 - self.b0))
        return (g, send(out, 4)), out

    def z2(self, g, r):
        b0, b1 = self.b0, self.b1
        out = pick(g, b0, 1 - b1) + pick(r, 1 - b1)
        keep = pick(g, b0, b1) + pick(r, b1)
        out, keep = hold((out, keep))
        return (keep, send(out, 8)), out

    def s1(self, keep, r):
        return Plane.s1(self, hold((keep + r).reshape(2, 2, 2, self.rows // 32, self.cols)))

    def g1(self, g, rx, ry):
        w = hold(pick(g, self.x, self.y) + rx + ry)
        return (w, send(w, 1), send(w, 2)), w

    def z3(self, w, rx, ry, d0, d1):
        c = jnp.zeros((self.rows // 4, self.cols), w.dtype)
        c = hold(self.gather(c, w, rx, ry, d0, d1, 0, 0))
        return (c, send(c, 8)), c

    def z4(self, c, o):
        h = hold(both(self.b1, c, o))
        return (h, send(h, 4)), h

    def end(self, h, o):
        bufs, name, row0, col0 = self.home
        n = self.rows // 2
        for piece, b in ((h, self.b0), (o, 1 - self.b0)):
            bufs[name] = lax.dynamic_update_slice(bufs[name], piece.reshape(n, self.cols), (row0 + b * n, col0))
        bufs[name] = hold(bufs[name])
        return (), bufs[name]


def swap(a):
    return lax.ppermute(a, "tensor", [(0, 1), (1, 0)])


class Block:
    def __init__(self, args):
        (self.tokens, self.cot, w_qkv, qv_bias, self.w_proj, proj_bias, self.w_fc1, fc1_bias, self.w_fc2, fc2_bias,
         gain_one, shift_one, gain_two, shift_two, rel_h, rel_w) = args
        self.rows, self.width = self.tokens.shape
        self.local = w_qkv.shape[2]
        self.units = self.w_fc1.shape[1] // 2
        self.rel_shape = rel_h.shape
        index = lax.axis_index("dp")
        self.first = jnp.reshape(index * (self.rows // TOK), (1,)).astype(jnp.int32)
        self.bits = tuple((index >> b) & 1 for b in range(4))
        line = lambda v: v.astype(F32)[None]
        self.g1, self.s1, self.g2, self.s2 = line(gain_one), line(shift_one), line(gain_two), line(shift_two)
        self.pb, self.b1, self.b2 = line(proj_bias), line(fc1_bias), line(fc2_bias)
        self.w3 = jnp.transpose(w_qkv, (1, 0, 2))
        bias = qv_bias.astype(F32)
        self.bias3 = jnp.stack([bias[0], jnp.zeros_like(bias[0]), bias[1]])
        relm = rel_matrix(rel_h, rel_w)
        self.rel_fwd = jnp.concatenate([relm, jnp.roll(relm, -8, axis=1)], 1)
        self.rel_bwd = jnp.concatenate([relm, relm], 1)
        self.once, self.hot = key_matrix()
        self.tab, self.spots = shift_table(), place_table()
        self.bufs = {
            "fc2": jnp.zeros((2 * self.units, self.width), F32),
            "fc1": jnp.zeros((self.width, 2 * self.units), F32),
            "qkv": jnp.zeros((3 * self.width, self.local), F32),
            "rest": jnp.zeros((self.local + 64, self.width), F32),
        }
        self.grads = {}

    def K1(self, token):
        other = swap(self.w_proj.astype(F32))
        self.hid1, self.low, self.qkv, self.prob, self.ctx, self.d_fc2_bias = attention_forward(
            self.first, self.tokens, self.cot, self.spots, self.g1, self.s1, self.w3, self.bias3, self.rel_fwd,
            self.hot, self.once, self.tab)
        self.ctx_other, self.proj_other = swap(self.ctx), other
        return self.ctx

    def K2a(self, token):
        ctx = wait_for(self.ctx, token)
        self.y, self.hid2, self.act0, self.pre0, self.sum0 = mlp_first(
            self.tokens, ctx, self.ctx_other, self.low, self.w_proj, self.proj_other, self.pb, self.g2, self.s2,
            self.w_fc1, self.b1, self.w_fc2)
        return self.hid2

    def K2b(self, token):
        hid = wait_for(self.hid2, token)
        self.act1, self.pre1, self.sum1 = mlp_second(hid, self.low, self.w_fc1, self.b1, self.w_fc2)
        return self.act1

    def grad(self, name, a, b, token):
        a = wait_for(a, token)
        self.grads[name] = hold(mm(a, b, TN))
        return self.grads[name]

    def dw2a(self, token):
        return self.grad("A0", self.act0, self.low, token)

    def dw2b(self, token):
        return self.grad("A1", self.act1, self.low, token)

    def dw2(self, token):
        low = wait_for(self.low, token)
        self.grads["A"] = hold(jnp.concatenate([mm(self.act0, low, TN), mm(self.act1, low, TN)], 0))
        return self.grads["A"]

    def dw1a(self, token):
        return self.grad("B0", self.hid2, self.pre0, token)

    def dw1b(self, token):
        return self.grad("B1", self.hid2, self.pre1, token)

    def dh2(self, token):
        pre = wait_for(self.pre0, token)
        n = self.units
        part = hold(mm(pre, self.w_fc1[:, :n], NT) + mm(self.pre1, self.w_fc1[:, n:], NT))
        self.dh2_part, self.dh2_other = part, swap(part)
        return part

    def fc2(self, token):
        act = wait_for(self.act0, token)
        n = self.units
        part = hold(mm(act, self.w_fc2[:n]) + mm(self.act1, self.w_fc2[n:]))
        self.fc2_part, self.fc2_other = part, swap(part)
        return part

    def K3(self, token):
        y = wait_for(self.y, token)
        self.dy, self.d_attn, self.dctx, self.sum_two = norm_two_back(
            self.dh2_part, self.dh2_other, y, self.low, self.g2, self.w_proj)
        return self.dctx

    def K4a(self, token):
        dctx = wait_for(self.dctx, token)
        self.dqkv, self.acc0, self.bias0 = attention_backward(
            dctx, self.qkv, self.prob, self.rel_bwd, self.once, self.tab, 0, 2)
        return self.acc0

    def K4b(self, token):
        dctx = wait_for(self.dctx, token)
        self.dqkv, acc, bias = attention_backward(
            dctx, self.qkv, self.prob, self.rel_bwd, self.once, self.tab, 1, 2, self.dqkv)
        self.acc = hold(self.acc0 + acc)
        self.acc_other = swap(self.acc)
        self.bias_qv = self.bias0 + bias
        return self.acc

    def dwq(self, token):
        hid = wait_for(self.hid1, token)
        self.grads["C"] = hold(jnp.concatenate([mm(hid, self.dqkv[t], TN) for t in range(3)], 0))
        return self.grads["C"]

    def dh1(self, token):
        d = wait_for(self.dqkv, token)
        part = hold(mm(d[0], self.w3[0], NT) + mm(d[1], self.w3[1], NT) + mm(d[2], self.w3[2], NT))
        self.dh1_part, self.dh1_other = part, swap(part)
        return part

    def dproj(self, token):
        attn = wait_for(self.d_attn, token)
        self.d_proj = hold(mm(self.ctx.astype(BF16), attn, TN))
        return self.d_proj

    def K5(self, token):
        dy = wait_for(self.dy, token)
        self.d_tokens, sum_one = norm_one_back(
            self.first, self.dh1_part, self.dh1_other, self.tokens, dy, self.spots, self.g1)
        rel_h, rel_w = split_rel(self.acc + self.acc_other)
        self.small = [
            sum_one[0], sum_one[1], self.sum_two[0], self.sum_two[1], self.sum_two[2], self.d_fc2_bias[0],
            self.sum0[0], self.sum1[0], self.bias_qv[0], self.bias_qv[2], rel_h.reshape(-1), rel_w.reshape(-1)]
        flat = jnp.concatenate(self.small)
        flat = jnp.pad(flat, (0, 64 * self.width - flat.shape[0])).reshape(64, self.width)
        self.flat = flat
        return self.d_tokens

    def K6(self, token):
        y = wait_for(self.y, token)
        self.output = block_output(self.first, self.fc2_part, self.fc2_other, y, self.spots, self.b2)
        return self.output

    def rest(self):
        self.grads["D"] = jnp.concatenate([self.d_proj, self.flat], 0)

    def results(self):
        n = self.local
        cuts, at = [], 0
        flat = self.bufs["rest"][n:].reshape(-1)
        for a in self.small:
            cuts.append(flat[at:at + a.shape[0]])
            at += a.shape[0]
        gain1, shift1, gain2, shift2, projb, fc2b, b1a, b1b, qb, vb, rel_h, rel_w = cuts
        dw_qkv = jnp.transpose(self.bufs["qkv"].reshape(3, self.width, n), (1, 0, 2))
        return (self.output, self.d_tokens, dw_qkv, jnp.stack([qb, vb]), self.bufs["rest"][:n], projb,
                self.bufs["fc1"], jnp.concatenate([b1a, b1b]), self.bufs["fc2"], fc2b, gain1, shift1, gain2, shift2,
                rel_h.reshape(self.rel_shape), rel_w.reshape(self.rel_shape))


def homes(block):
    u = block.units
    return {"A": ("fc2", 0, 0), "A0": ("fc2", 0, 0), "A1": ("fc2", u, 0), "B0": ("fc1", 0, 0), "B1": ("fc1", 0, u),
            "C": ("qkv", 0, 0), "D": ("rest", 0, 0)}


ORDER = (
    "K1", "K2a", "K2b", "dw2", "A.s1", "dw1b", "dw1a", "dh2", "B1.s1", "B0.z1", "A.s2", "K3", "K4a", "B1.s2", "B0.z2", "A.z1", "K4b", "dwq", "C.s1", "B1.z1", "A.z2",
    "dh1", "B0.s1", "B1.z2", "C.s2", "A.z3", "K5", "dproj", "B0.s2", "B1.z3", "D.s1", "A.z4", "C.z1", "B0.g1", "D.s2", "B0.g2", "A.g1", "B1.z4", "D.z1", "C.z2",
    "fc2", "B1.g1", "D.z2", "C.z3", "D.z3", "B0.z3", "A.g2", "D.z4", "B1.g2", "C.z4", "D.g1", "C.g1", "B0.z4", "D.g2", "K6", "B1.end", "A.end", "C.g2", "D.end",
    "B0.end", "C.end",
)
COLUMNS = ('B0',)


def shards(*args):
    block = Block(args)
    where = homes(block)
    token, sums, ordered = None, {}, lax.axis_size("dp") == 16
    for item in ORDER:
        if "." not in item:
            token = getattr(block, item)(token)
            continue
        if not ordered:
            continue
        name, step = item.split(".")
        if name not in sums:
            if name == "D":
                block.rest()
            kind = Column if name in COLUMNS else Plane
            sums[name] = kind(block.grads[name], block.bits, (block.bufs,) + where[name])
        token = sums[name].step(step, token)
    if not ordered:
        block.rest()
        total = lax.psum(block.grads, "dp")
        for name, g in total.items():
            buf, row, col = where[name]
            block.bufs[buf] = lax.dynamic_update_slice(block.bufs[buf], g, (row, col))
    return block.results()


def solution(mesh):
    rows, rep = P("dp", None), P()
    ins = (rows, rows, P(None, None, "tensor"), P(None, "tensor"), P("tensor", None), rep, P(None, "tensor"),
           P("tensor"), P("tensor", None), rep, rep, rep, rep, rep, rep, rep)
    return jax.shard_map(shards, mesh=mesh, in_specs=ins, out_specs=ins, check_vma=False)
```

time: 554 us -> 497 us (0.90)
  the two profiles are of different devices: /device:TPU:0 before, /device:TPU:16 now
where the time goes in v2:
time: 497 us; the launch traced here: 489 us
  waiting for transfers between devices  139 us (28%)
  Pallas kernels  104 us (21%)
  starting transfers between devices  89.6 us (18%)
  local copies, waits for them, and re-layouts  82.6 us (17%)
  matrix products  42.6 us (9%)
  other arithmetic  28.8 us (6%)
    ppermute x60, waiting for transfers between devices, send(): return lax.ppermute(a, 'dp', [(i, i ^ stride) for i in range(n)])  129 us
    ppermute x60, starting transfers between devices, send(): return lax.ppermute(a, 'dp', [(i, i ^ stride) for i in range(n)])  88.8 us
    dot_general x15, matrix products, mm(): return lax.dot_general(a, b, dims, preferred_element_type=F32)  42.6 us
    pallas_call x2, Pallas kernels, attention_backward(): pl.pallas_call(kernel, grid=(steps,), input_output_aliases={} if done is...  28.8 us
    pallas_call x1, Pallas kernels, attention_forward(): pl.pallas_call(fwd_kernel, grid=(steps,), in_specs=[pl.BlockSpec(memory_s...  25.6 us
    unnamed x122, local copies, waits for them, and re-layouts  20.6 us
    dynamic_update_slice x25, local copies, waits for them, and re-layouts, gather(): lax.dynamic_update_slice(out, piece, (row0 + (2 * px + py) * slab + off,...  17 us
    pallas_call x1, Pallas kernels, mlp_first(): pl.pallas_call(mlp_first_kernel, grid=(rows // (2 * TOK),), in_specs=[row...  15.2 us
  transfers between devices with their start and end apart: 66, of which 26 were waited for; matrix products, arithmetic and copies ran while one was open for 18% of the time, Pallas kernels for 8%

profile of v2, /device:TPU:16, one launch (start us, length us, event | category | flops | bytes accessed | tf_op | source)
XLA Modules:
  0.0 488.7 jit_solution(12358111159643696445)
XLA Ops:
  10.0 25.6 %attention_forward.1 = (bf16[1568,768]{1,0:T(8,128)(2,1)S(1)}, bf16[1568,768]{1,0:T(8,128)(2,1)}, bf16[8,208,1152]{2,1,0:T(8,128)(2,1)}, bf16[8,6,208,208]{3,2,1...) custom-call(s32[1]{0:T(128)} %bitcast.first_ref, bf16[1568,768]{1,0:T(8,128)(2,1)} %tok_ref.3, ...), custom_call_target="tpu_custom_call" | custom-call | flops 3776446464 | bytes 21012480 | tf_op jit(solution)/shard_map/attention_forward/pallas_call | solution.py:144
  37.8 5.4 %collective-permute-done.1.wpo_ref = f32[384,768]{1,0:T(8,128)S(1)} collective-permute-done((f32[384,768]{1,0:T(8,128)S(1)}, f32[384,768]{1,0:T(8,128)S(1)}, u32[]{:S(2)}, u32[]{:S(2)}) %collective-permute-start.1) | collective-permute-done | bytes 1179680 | tf_op jit(solution)/shard_map/ppermute | solution.py:606
  47.1 15.2 %mlp_first.1 = (f32[1568,768]{1,0:T(8,128)}, bf16[1568,768]{1,0:T(8,128)(2,1)}, bf16[1568,768]{1,0:T(8,128)(2,1)}, bf16[1568,768]{1,0:T(8,128)(2,1)}, f32[1,768]{1,0:T(1,128)S(1)}) custom-call(bf16[1568,768]{1,0:T(8,128)(2,1)} %tok_ref.3, f32[1568,384]{1,0:T(8,128)} %get-tuple-element.221.ctx_ref, f32[1568,384]{1,0:T(8,128)} %collective-permute-done.oth_ref, ...), custom_call_target="tpu_custom_call" | custom-call | flops 5549064192 | bytes 21676032 | tf_op jit(solution)/shard_map/mlp_first/pallas_call | solution.py:328
  62.3 8.0 %mlp_second.1 = (bf16[1568,768]{1,0:T(8,128)(2,1)}, bf16[1568,768]{1,0:T(8,128)(2,1)}, f32[1,768]{1,0:T(1,128)S(1)}) custom-call(bf16[1568,768]{1,0:T(8,128)(2,1)} %get-tuple-element.234.hid_ref, bf16[1568,768]{1,0:T(8,128)(2,1)} %get-tuple-element.229.low_ref, bf16[768,1536]{1,0:T(8,128)(2,1)S(1)} %copy-done.10, f32[1,1536]{1,0:T(1,128)S(1)} %reshape.549.b1_ref, ...), custom_call_target="tpu_custom_call" | custom-call | flops 3699376128 | bytes 9633792 | tf_op jit(solution)/shard_map/mlp_second/pallas_call | solution.py:354
  91.3 4.6 convolution_add_fusion.1.part_ref
  104.9 6.9 %collective-permute-done.3 = f32[192,768]{1,0:T(8,128)S(1)} collective-permute-done((f32[192,768]{1,0:T(8,128)}, f32[192,768]{1,0:T(8,128)S(1)}, u32[]{:S(2)}, u32[]{:S(2)}) %collective-permute-start.3) | collective-permute-done | bytes 589856 | tf_op jit(solution)/shard_map/ppermute | solution.py:467
  122.5 10.0 %norm_two_back.1 = (f32[1568,768]{1,0:T(8,128)}, bf16[1568,768]{1,0:T(8,128)(2,1)S(1)}, f32[1568,384]{1,0:T(8,128)S(1)}, f32[8,768]{1,0:T(8,128)S(1)}) custom-call(f32[1568,768]{1,0:T(8,128)} %convolution_add_fusion.1.part_ref, f32[1568,768]{1,0:T(8,128)} %collective-permute-done.2.oth_ref, f32[1568,768]{1,0:T(8,128)} %get-tuple-element.390.y_ref, ...), custom_call_target="tpu_custom_call" | custom-call | flops 924844032 | bytes 26492928 | tf_op jit(solution)/shard_map/norm_two_back/pallas_call | solution.py:397
  132.5 14.2 %attention_backward.2 = (bf16[3,1568,384]{2,1,0:T(8,128)(2,1)}, f32[128,256]{1,0:T(8,128)S(1)}, f32[8,384]{1,0:T(8,128)S(1)}) custom-call(f32[1568,384]{1,0:T(8,128)S(1)} %get-tuple-element.264.dctx_ref, bf16[8,208,1152]{2,1,0:T(8,128)(2,1)} %get-tuple-element.248.qkv_ref, bf16[8,6,208,208]{3,2,1,0:T(8,128)(2,1)} %get-tuple-element.249.prob_ref, ...), custom_call_target="tpu_custom_call" | custom-call | flops 1502871552 | bytes 8097792 | tf_op jit(solution)/shard_map/attention_backward/pallas_call | solution.py:237
  146.8 5.4 %collective-permute-done.8 = f32[96,768]{1,0:T(8,128)S(1)} collective-permute-done((f32[96,768]{1,0:T(8,128)}, f32[96,768]{1,0:T(8,128)S(1)}, u32[]{:S(2)}, u32[]{:S(2)}) %collective-permute-start.8) | collective-permute-done | bytes 294944 | tf_op jit(solution)/shard_map/ppermute | solution.py:467
  161.0 14.6 %attention_backward.3 = (bf16[3,1568,384]{2,1,0:T(8,128)(2,1)}, f32[128,256]{1,0:T(8,128)S(1)}, f32[8,384]{1,0:T(8,128)S(1)}) custom-call(f32[1568,384]{1,0:T(8,128)S(1)} %get-tuple-element.264.dctx_ref, bf16[8,208,1152]{2,1,0:T(8,128)(2,1)} %get-tuple-element.248.qkv_ref, ...), custom_call_target="tpu_custom_call", output_to_operand_aliasing={{0}: (6, {})} | custom-call | flops 1502871552 | bytes 8097792 | tf_op jit(solution)/shard_map/attention_backward/pallas_call | solution.py:237
  187.6 8.8 %collective-permute-done.12 = f32[2,96,768]{2,1,0:T(8,128)S(1)} collective-permute-done((f32[2,96,768]{2,1,0:T(8,128)}, f32[2,96,768]{2,1,0:T(8,128)S(1)}, u32[]{:S(2)}, u32[]{:S(2)}) %collective-permute-start.12) | collective-permute-done | bytes 589856 | tf_op jit(solution)/shard_map/ppermute | solution.py:467
  209.7 5.0 %collective-permute-done.22 = f32[128,256]{1,0:T(8,128)S(1)} collective-permute-done((f32[128,256]{1,0:T(8,128)}, f32[128,256]{1,0:T(8,128)S(1)}, u32[]{:S(2)}, u32[]{:S(2)}) %collective-permute-start.22) | collective-permute-done | bytes 131104 | tf_op jit(solution)/shard_map/ppermute | solution.py:606
  216.7 16.1 %collective-permute-done.15 = f32[192,768]{1,0:T(8,128)S(1)} collective-permute-done((f32[192,768]{1,0:T(8,128)}, f32[192,768]{1,0:T(8,128)S(1)}, u32[]{:S(2)}, u32[]{:S(2)}) %collective-permute-start.15) | collective-permute-done | bytes 589856 | tf_op jit(solution)/shard_map/ppermute | solution.py:467
  247.2 5.7 %collective-permute-done.19 = f32[96,768]{1,0:T(8,128)S(1)} collective-permute-done((f32[96,768]{1,0:T(8,128)}, f32[96,768]{1,0:T(8,128)S(1)}, u32[]{:S(2)}, u32[]{:S(2)}) %collective-permute-start.19) | collective-permute-done | bytes 294944 | tf_op jit(solution)/shard_map/ppermute | solution.py:467
  257.7 8.7 %norm_one_back.1 = (bf16[1568,768]{1,0:T(8,128)(2,1)}, f32[8,768]{1,0:T(8,128)S(1)}) custom-call(s32[1]{0:T(128)} %bitcast.first_ref, f32[1568,768]{1,0:T(8,128)} %add_add_fusion.part_ref, f32[1568,768]{1,0:T(8,128)} %collective-permute-done.21.oth_ref, bf16[1568,768]{1,0:T(8,128)(2,1)S(1)} %copy-done, f32[1568,768]{1,0:T(8,128)} %get-tuple-element.300.dy_ref, ...), custom_call_target="tpu_custom_call" | custom-call | flops 24084480 | bytes 19267584 | tf_op jit(solution)/shard_map/norm_one_back/pallas_call | solution.py:425
  279.2 12.4 %collective-permute-done.18 = f32[2,288,384]{2,1,0:T(8,128)} collective-permute-done((f32[2,288,384]{2,1,0:T(8,128)}, f32[2,288,384]{2,1,0:T(8,128)}, u32[]{:S(2)}, u32[]{:S(2)}) %collective-permute-start.18) | collective-permute-done | bytes 884768 | tf_op jit(solution)/shard_map/ppermute | solution.py:467
  358.9 5.2 %collective-permute-done.42 = f32[56,384]{1,0:T(8,128)S(1)} collective-permute-done((f32[56,384]{1,0:T(8,128)S(1)}, f32[56,384]{1,0:T(8,128)S(1)}, u32[]{:S(2)}, u32[]{:S(2)}) %collective-permute-start.42) | collective-permute-done | bytes 86048 | tf_op jit(solution)/shard_map/ppermute | solution.py:467
  371.9 13.7 %collective-permute-start.47 = (f32[56,768]{1,0:T(8,128)S(1)}, f32[56,768]{1,0:T(8,128)S(1)}, u32[]{:S(2)}, u32[]{:S(2)}) collective-permute-start(f32[56,768]{1,0:T(8,128)S(1)} %bitcast.403), channel_id=1, source_target_pairs={{0,8},{2,10},{4,12},{6,14},{8,0},{10,2},{12,4},{14,6},{16,24},{18,... | collective-permute-start | bytes 516104 | tf_op jit(solution)/shard_map/ppermute | solution.py:467
  389.5 9.2 %collective-permute-done.47 = f32[56,768]{1,0:T(8,128)S(1)} collective-permute-done((f32[56,768]{1,0:T(8,128)S(1)}, f32[56,768]{1,0:T(8,128)S(1)}, u32[]{:S(2)}, u32[]{:S(2)}) %collective-permute-start.47) | collective-permute-done | bytes 172064 | tf_op jit(solution)/shard_map/ppermute | solution.py:467
  401.3 10.3 %collective-permute-done.54 = f32[288,384]{1,0:T(8,128)S(1)} collective-permute-done((f32[288,384]{1,0:T(8,128)S(1)}, f32[288,384]{1,0:T(8,128)S(1)}, u32[]{:S(2)}, u32[]{:S(2)}) %collective-permute-start.54) | collective-permute-done | bytes 442400 | tf_op jit(solution)/shard_map/ppermute | solution.py:467
  415.4 5.6 %collective-permute-done.51 = f32[2,56,768]{2,1,0:T(8,128)S(1)} collective-permute-done((f32[2,56,768]{2,1,0:T(8,128)S(1)}, f32[2,56,768]{2,1,0:T(8,128)S(1)}, u32[]{:S(2)}, u32[]{:S(2)}) %collective-permute-start.51) | collective-permute-done | bytes 344096 | tf_op jit(solution)/shard_map/ppermute | solution.py:467
  424.4 7.3 %block_output.1 = bf16[1568,768]{1,0:T(8,128)(2,1)} custom-call(s32[1]{0:T(128)} %bitcast.first_ref, f32[1568,768]{1,0:T(8,128)} %convolution_add_fusion.part_ref, f32[1568,768]{1,0:T(8,128)} %collective-permute-done.37.oth_ref, f32[1568,768]{1,0:T(8,128)} %get-tuple-element.390.y_ref, f32[392,128]{1,0:T(8,128)S(1)} %copy-done.5, f32[1,768]{1,0:T(1,128)S(1)} %reshape.550.bias_ref), custom_call_target="tpu_custom_call" | custom-call | flops 4816896 | bytes 16859136 | tf_op jit(solution)/shard_map/block_output/pallas_call | solution.py:445
  447.8 14.2 %collective-permute-done.56 = f32[2,288,384]{2,1,0:T(8,128)S(1)} collective-permute-done((f32[2,288,384]{2,1,0:T(8,128)S(1)}, f32[2,288,384]{2,1,0:T(8,128)S(1)}, u32[]{:S(2)}, u32[]{:S(2)}) %collective-permute-start.56) | collective-permute-done | bytes 884768 | tf_op jit(solution)/shard_map/ppermute | solution.py:467
  478.2 5.9 %collective-permute-done.62 = f32[288,384]{1,0:T(8,128)S(1)} collective-permute-done((f32[288,384]{1,0:T(8,128)S(1)}, f32[288,384]{1,0:T(8,128)S(1)}, u32[]{:S(2)}, u32[]{:S(2)}) %collective-permute-start.62) | collective-permute-done | bytes 442400 | tf_op jit(solution)/shard_map/ppermute | solution.py:467
  (420 shorter events, 248.7 us)
Async XLA Ops:
  103.3 53.0 %collective-permute-start.7 = (f32[2,192,768]{2,1,0:T(8,128)}, f32[2,192,768]{2,1,0:T(8,128)}, u32[]{:S(2)}, u32[]{:S(2)}) collective-permute-start(f32[2,192,768]{2,1,0:T(8,128)} %dynamic-slice_bitcast_fusion), channel_id=1, source_target_pairs={{0,8},{2,10},{4,12},{6,14},{8,0},{10,2},{12,4},{14,6},{16,24},{18,... | collective-permute-start | bytes 3538952 | tf_op jit(solution)/shard_map/ppermute | solution.py:467
  118.5 40.3 %collective-permute-start.5 = (f32[2,192,768]{2,1,0:T(8,128)}, f32[2,192,768]{2,1,0:T(8,128)}, u32[]{:S(2)}, u32[]{:S(2)}) collective-permute-start(f32[2,192,768]{2,1,0:T(8,128)} %get-tuple-element.244), channel_id=1, source_target_pairs={{0,2},{2,0},{4,6},{6,4},{8,10},{10,8},{12,14},{14,12},{16,18},{18,... | collective-permute-start | bytes 3538952 | tf_op jit(solution)/shard_map/ppermute | solution.py:467
  119.6 39.2 %collective-permute-start.6 = (f32[2,192,768]{2,1,0:T(8,128)}, f32[2,192,768]{2,1,0:T(8,128)}, u32[]{:S(2)}, u32[]{:S(2)}) collective-permute-start(f32[2,192,768]{2,1,0:T(8,128)} %get-tuple-element.251), channel_id=1, source_target_pairs={{0,4},{2,6},{4,0},{6,2},{8,12},{10,14},{12,8},{14,10},{16,20},{18,... | collective-permute-start | bytes 3538952 | tf_op jit(solution)/shard_map/ppermute | solution.py:467
  121.1 31.1 %collective-permute-start.8 = (f32[96,768]{1,0:T(8,128)}, f32[96,768]{1,0:T(8,128)S(1)}, u32[]{:S(2)}, u32[]{:S(2)}) collective-permute-start(f32[96,768]{1,0:T(8,128)} %get-tuple-element.239), channel_id=1, source_target_pairs={{0,2},{2,0},{4,6},{6,4},{8,10},{10,8},{12,14},{14,12},{16,18},{18,... | collective-permute-start | bytes 884744 | tf_op jit(solution)/shard_map/ppermute | solution.py:467
  122.0 31.4 %collective-permute-start.9 = (f32[96,768]{1,0:T(8,128)}, f32[96,768]{1,0:T(8,128)}, u32[]{:S(2)}, u32[]{:S(2)}) collective-permute-start(f32[96,768]{1,0:T(8,128)} %get-tuple-element.252), channel_id=1, source_target_pairs={{0,4},{2,6},{4,0},{6,2},{8,12},{10,14},{12,8},{14,10},{16,20},{18,... | collective-permute-start | bytes 884744 | tf_op jit(solution)/shard_map/ppermute | solution.py:467
  206.2 50.1 %collective-permute-start.21 = (f32[1568,768]{1,0:T(8,128)}, f32[1568,768]{1,0:T(8,128)}, u32[]{:S(2)}, u32[]{:S(2)}) collective-permute-start(f32[1568,768]{1,0:T(8,128)} %add_add_fusion.part_ref), channel_id=1, source_target_pairs={{0,1},{1,0},{2,3},{3,2},{4,5},{5,4},{6,7},{7,6},{8,9},{9,8},{10,11... | collective-permute-start | bytes 14450696 | tf_op jit(solution)/shard_map/ppermute | solution.py:606
  206.7 34.2 %collective-permute-start.10 = (f32[288,384]{1,0:T(8,128)}, f32[288,384]{1,0:T(8,128)}, u32[]{:S(2)}, u32[]{:S(2)}) collective-permute-start(f32[288,384]{1,0:T(8,128)} %get-tuple-element.270), channel_id=1, source_target_pairs={{0,2},{2,0},{4,6},{6,4},{8,10},{10,8},{12,14},{14,12},{16,18},{18,... | collective-permute-start | bytes 1327112 | tf_op jit(solution)/shard_map/ppermute | solution.py:467
  208.1 34.3 %collective-permute-start.11 = (f32[288,384]{1,0:T(8,128)}, f32[288,384]{1,0:T(8,128)}, u32[]{:S(2)}, u32[]{:S(2)}) collective-permute-start(f32[288,384]{1,0:T(8,128)} %get-tuple-element.271), channel_id=1, source_target_pairs={{0,4},{2,6},{4,0},{6,2},{8,12},{10,14},{12,8},{14,10},{16,20},{18,... | collective-permute-start | bytes 1327112 | tf_op jit(solution)/shard_map/ppermute | solution.py:467
  238.3 30.5 %collective-permute-start.24 = (f32[24,768]{1,0:T(8,128)S(1)}, f32[24,768]{1,0:T(8,128)S(1)}, u32[]{:S(2)}, u32[]{:S(2)}) collective-permute-start(f32[24,768]{1,0:T(8,128)S(1)} %get-tuple-element.286), channel_id=1, source_target_pairs={{0,2},{2,0},{4,6},{6,4},{8,10},{10,8},{12,14},{14,12},{16,18},{18,... | collective-permute-start | bytes 221192 | tf_op jit(solution)/shard_map/ppermute | solution.py:467
  240.9 29.5 %collective-permute-start.25 = (f32[24,768]{1,0:T(8,128)S(1)}, f32[24,768]{1,0:T(8,128)S(1)}, u32[]{:S(2)}, u32[]{:S(2)}) collective-permute-start(f32[24,768]{1,0:T(8,128)S(1)} %get-tuple-element.311), channel_id=1, source_target_pairs={{0,4},{2,6},{4,0},{6,2},{8,12},{10,14},{12,8},{14,10},{16,20},{18,... | collective-permute-start | bytes 221192 | tf_op jit(solution)/shard_map/ppermute | solution.py:467
  242.5 30.1 %collective-permute-start.23 = (f32[48,768]{1,0:T(8,128)S(1)}, f32[48,768]{1,0:T(8,128)S(1)}, u32[]{:S(2)}, u32[]{:S(2)}) collective-permute-start(f32[48,768]{1,0:T(8,128)S(1)} %get-tuple-element.289), channel_id=1, source_target_pairs={{0,16},{2,18},{4,20},{6,22},{8,24},{10,26},{12,28},{14,30},{16,0},... | collective-permute-start | bytes 442376 | tf_op jit(solution)/shard_map/ppermute | solution.py:467
  279.2 31.0 %collective-permute-start.33 = (f32[48,768]{1,0:T(8,128)S(1)}, f32[48,768]{1,0:T(8,128)S(1)}, u32[]{:S(2)}, u32[]{:S(2)}) collective-permute-start(f32[48,768]{1,0:T(8,128)S(1)} %add.582), channel_id=1, source_target_pairs={{0,16},{2,18},{4,20},{6,22},{8,24},{10,26},{12,28},{14,30},{16,0},... | collective-permute-start | bytes 442376 | tf_op jit(solution)/shard_map/ppermute | solution.py:467
  320.8 31.2 %collective-permute-start.43 = (f32[2,192,768]{2,1,0:T(8,128)S(1)}, f32[2,192,768]{2,1,0:T(8,128)S(1)}, u32[]{:S(2)}, u32[]{:S(2)}) collective-permute-start(f32[2,192,768]{2,1,0:T(8,128)S(1)} %bitcast_dynamic-update-slice_fusion.2), channel_id=1, source_target_pairs={{0,2},{2,0},{4,6},{6,4},{8,10},{10,8},{12,14},{14,12},{16,18},{18,... | collective-permute-start | bytes 3538952 | tf_op jit(solution)/shard_map/ppermute | solution.py:467
  321.5 34.6 %collective-permute-start.44 = (f32[2,192,768]{2,1,0:T(8,128)S(1)}, f32[2,192,768]{2,1,0:T(8,128)}, u32[]{:S(2)}, u32[]{:S(2)}) collective-permute-start(f32[2,192,768]{2,1,0:T(8,128)S(1)} %bitcast_dynamic-update-slice_fusion.2), channel_id=1, source_target_pairs={{0,4},{2,6},{4,0},{6,2},{8,12},{10,14},{12,8},{14,10},{16,20},{18,... | collective-permute-start | bytes 3538952 | tf_op jit(solution)/shard_map/ppermute | solution.py:467
  329.5 93.6 %collective-permute-start.37 = (f32[1568,768]{1,0:T(8,128)}, f32[1568,768]{1,0:T(8,128)}, u32[]{:S(2)}, u32[]{:S(2)}) collective-permute-start(f32[1568,768]{1,0:T(8,128)} %convolution_add_fusion.part_ref), channel_id=1, source_target_pairs={{0,1},{1,0},{2,3},{3,2},{4,5},{5,4},{6,7},{7,6},{8,9},{9,8},{10,11... | collective-permute-start | bytes 14450696 | tf_op jit(solution)/shard_map/ppermute | solution.py:606
  340.9 29.7 %collective-permute-start.49 = (f32[2,96,768]{2,1,0:T(8,128)S(1)}, f32[2,96,768]{2,1,0:T(8,128)}, u32[]{:S(2)}, u32[]{:S(2)}) collective-permute-start(f32[2,96,768]{2,1,0:T(8,128)S(1)} %bitcast_dynamic-update-slice_fusion.6), channel_id=1, source_target_pairs={{0,2},{2,0},{4,6},{6,4},{8,10},{10,8},{12,14},{14,12},{16,18},{18,... | collective-permute-start | bytes 1769480 | tf_op jit(solution)/shard_map/ppermute | solution.py:467
  341.8 30.1 %collective-permute-start.50 = (f32[2,96,768]{2,1,0:T(8,128)S(1)}, f32[2,96,768]{2,1,0:T(8,128)}, u32[]{:S(2)}, u32[]{:S(2)}) collective-permute-start(f32[2,96,768]{2,1,0:T(8,128)S(1)} %bitcast_dynamic-update-slice_fusion.6), channel_id=1, source_target_pairs={{0,4},{2,6},{4,0},{6,2},{8,12},{10,14},{12,8},{14,10},{16,20},{18,... | collective-permute-start | bytes 1769480 | tf_op jit(solution)/shard_map/ppermute | solution.py:467
  352.0 35.7 %collective-permute-start.48 = (f32[144,384]{1,0:T(8,128)S(1)}, f32[144,384]{1,0:T(8,128)}, u32[]{:S(2)}, u32[]{:S(2)}) collective-permute-start(f32[144,384]{1,0:T(8,128)S(1)} %add.606), channel_id=1, source_target_pairs={{0,16},{2,18},{4,20},{6,22},{8,24},{10,26},{12,28},{14,30},{16,0},... | collective-permute-start | bytes 663560 | tf_op jit(solution)/shard_map/ppermute | solution.py:467
  364.1 48.9 %collective-permute-start.53 = (f32[192,768]{1,0:T(8,128)}, f32[192,768]{1,0:T(8,128)}, u32[]{:S(2)}, u32[]{:S(2)}) collective-permute-start(f32[192,768]{1,0:T(8,128)} %constant_dynamic-update-slice_fusion.10), channel_id=1, source_target_pairs={{0,16},{2,18},{4,20},{6,22},{8,24},{10,26},{12,28},{14,30},{16,0},... | collective-permute-start | bytes 1769480 | tf_op jit(solution)/shard_map/ppermute | solution.py:467
  370.6 72.3 %collective-permute-start.57 = (f32[192,768]{1,0:T(8,128)}, f32[192,768]{1,0:T(8,128)S(1)}, u32[]{:S(2)}, u32[]{:S(2)}) collective-permute-start(f32[192,768]{1,0:T(8,128)} %slice_bitcast_fusion.7), channel_id=1, source_target_pairs={{0,2},{2,0},{4,6},{6,4},{8,10},{10,8},{12,14},{14,12},{16,18},{18,... | collective-permute-start | bytes 1769480 | tf_op jit(solution)/shard_map/ppermute | solution.py:467
  371.9 26.8 %collective-permute-start.47 = (f32[56,768]{1,0:T(8,128)S(1)}, f32[56,768]{1,0:T(8,128)S(1)}, u32[]{:S(2)}, u32[]{:S(2)}) collective-permute-start(f32[56,768]{1,0:T(8,128)S(1)} %bitcast.403), channel_id=1, source_target_pairs={{0,8},{2,10},{4,12},{6,14},{8,0},{10,2},{12,4},{14,6},{16,24},{18,... | collective-permute-start | bytes 516104 | tf_op jit(solution)/shard_map/ppermute | solution.py:467
  387.7 44.1 %collective-permute-start.59 = (f32[96,768]{1,0:T(8,128)S(1)}, f32[96,768]{1,0:T(8,128)S(1)}, u32[]{:S(2)}, u32[]{:S(2)}) collective-permute-start(f32[96,768]{1,0:T(8,128)S(1)} %slice_bitcast_fusion.11), channel_id=1, source_target_pairs={{0,2},{2,0},{4,6},{6,4},{8,10},{10,8},{12,14},{14,12},{16,18},{18,... | collective-permute-start | bytes 884744 | tf_op jit(solution)/shard_map/ppermute | solution.py:467
  431.8 30.3 %collective-permute-start.56 = (f32[2,288,384]{2,1,0:T(8,128)S(1)}, f32[2,288,384]{2,1,0:T(8,128)S(1)}, u32[]{:S(2)}, u32[]{:S(2)}) collective-permute-start(f32[2,288,384]{2,1,0:T(8,128)S(1)} %bitcast_dynamic-update-slice_fusion.4), channel_id=1, source_target_pairs={{0,4},{2,6},{4,0},{6,2},{8,12},{10,14},{12,8},{14,10},{16,20},{18,... | collective-permute-start | bytes 2654216 | tf_op jit(solution)/shard_map/ppermute | solution.py:467
  432.5 39.4 %collective-permute-start.63 = (f32[2,192,768]{2,1,0:T(8,128)S(1)}, f32[2,192,768]{2,1,0:T(8,128)}, u32[]{:S(2)}, u32[]{:S(2)}) collective-permute-start(f32[2,192,768]{2,1,0:T(8,128)S(1)} %bitcast_dynamic-update-slice_fusion), channel_id=1, source_target_pairs={{0,8},{2,10},{4,12},{6,14},{8,0},{10,2},{12,4},{14,6},{16,24},{18,... | collective-permute-start | bytes 3538952 | tf_op jit(solution)/shard_map/ppermute | solution.py:467
  (101 other events, 1171.0 us)
